TPU v7x, 32 devices: a whole 2x2x4 slice. The times are simulated.
32 devices in a mesh: fsdp: 16 (over z, x, core), rep: 2 (over y).
Axes of the slice: x: 2, y: 2, z: 4, core: 2. Of those that a mesh axis runs over, the one named last changes fastest.
Arguments:
- tokens: bfloat16 [32768, 768], P(('fsdp', 'rep')), may hold values from -6 to 6
- w_qkv: bfloat16 [1769472], P('fsdp'), may hold values from -0.21875 to 0.21875
- w_out: bfloat16 [589824], P('fsdp'), may hold values from -0.875 to 0.875
- w_fc1: bfloat16 [2359296], P('fsdp'), may hold values from -0.21875 to 0.21875
- w_fc2: bfloat16 [2359296], P('fsdp'), may hold values from -0.109375 to 0.109375
- gains: bfloat16 [1536], P('fsdp'), may hold values from 0.099609375 to 1.8984375
- biases: bfloat16 [7680], P('fsdp'), may hold values from -3 to 3
- segment: int32 [32768], P(('fsdp', 'rep')), may hold values from 0 to 40, as said below
- cotangent: bfloat16 [32768, 768], P(('fsdp', 'rep')), may hold values from -6 to 6
Outputs:
- output: bfloat16 [32768, 768], P(('fsdp', 'rep'))
- grad_tokens: float32 [32768, 768], P(('fsdp', 'rep'))
- grad_qkv: float32 [1769472], P('fsdp')
- grad_out: float32 [589824], P('fsdp')
- grad_fc1: float32 [2359296], P('fsdp')
- grad_fc2: float32 [2359296], P('fsdp')
- grad_gains: float32 [1536], P('fsdp')
- grad_biases: float32 [7680], P('fsdp')
Inputs may be any that keep to these rules, and one draw needn't show every extreme that they name: Within the 1024 tokens of one device, segment numbers start at 0, never fall and rise by at most one from token to token, so every image lies whole on one device. Every image but the last of a device has 25, 64 or 900 tokens; the last image of each device may be cut short by the device's end to as few as 1 token and is still a segment of its own. Some device holds an image of exactly 900 tokens, and some device holds only images of 25 tokens apart from its cut last one.
All inputs are finite; a program needn't handle non-finite values.
Results may differ from a plain program's by a relative error of at most 0.013.
Values may be sent and summed in bfloat16 or wider, within the bound.
No kernel may reach another device: no remote copies, remote signals or barrier semaphores. Data moves between devices by JAX's collectives and lax.ppermute only.
A program may use at most 192 MiB of HBM per device.

v0:
```python
import functools

import jax
import jax.numpy as jnp
from jax import lax
from jax.experimental import pallas as pl
from jax.experimental.pallas import tpu as pltpu
from jax.sharding import Mesh
from jax.sharding import PartitionSpec as P

D = 768
H = 12
HD = 64
FF = 3072
B16 = jnp.bfloat16
F32 = jnp.float32

epsilon_norm = 1e-06
score_scale = 0.125
masked_low = -1e30

FWD_GROUPS = (4, 8)
NZ, NX = 4, 2
ROWS = D // 16
ROWS2 = FF // 16
FSDP = ("z", "x", "core")


def mm(a, b, ca, cb):
    return lax.dot_general(a, b, (((ca,), (cb,)), ((), ())), preferred_element_type=F32)


def params(mib=56):
    return pltpu.CompilerParams(
        dimension_semantics=("arbitrary",), vmem_limit_bytes=mib * 1024 * 1024
    )


def cost(flops, nbytes, trans=0):
    return pl.CostEstimate(flops=int(flops), bytes_accessed=int(nbytes), transcendentals=int(trans))


def shape(dims, dtype):
    return jax.ShapeDtypeStruct(dims, dtype)


def layer_norm(values, gain, shift):
    center = values - jnp.mean(values, axis=-1, keepdims=True)
    spread = jnp.mean(center * center, axis=-1, keepdims=True)
    return center * lax.rsqrt(spread + epsilon_norm) * gain + shift


def layer_norm_back(values, gain, grad):
    center = values - jnp.mean(values, axis=-1, keepdims=True)
    spread = jnp.mean(center * center, axis=-1, keepdims=True)
    inverse = lax.rsqrt(spread + epsilon_norm)
    hat = center * inverse
    grad_hat = grad * gain
    grad_values = inverse * (
        grad_hat
        - jnp.mean(grad_hat, axis=-1, keepdims=True)
        - hat * jnp.mean(grad_hat * hat, axis=-1, keepdims=True)
    )
    return grad_values, jnp.sum(grad * hat, axis=0, keepdims=True), jnp.sum(grad, axis=0, keepdims=True)


def normal(u):
    bell = jnp.exp(u * u * -0.5)
    t = 1.0 / (1.0 + 0.2316418882663604 * jnp.abs(u))
    top = 0.5307027145
    for c in (-0.7265760135, 0.7107068705, -0.142248368, 0.127414796):
        top = top * t + c
    tail = top * t * bell
    return jnp.where(u < 0.0, tail, 1.0 - tail), bell * 0.3989422804014327


def places(tab, rows):
    core = tab[8]
    for t in range(NZ * NX):
        base = tab[t] * 2
        yield (
            t,
            pl.ds(pl.multiple_of((base + core) * rows, 16), rows),
            pl.ds(pl.multiple_of((base + 1 - core) * rows, 16), rows),
        )


def assemble(tab, parts, dest):
    for t, here, there in places(tab, ROWS):
        rx, rz = divmod(t, NZ)
        dest[here, :] = parts[rx][rz]
        dest[there, :] = parts[2 + rx][rz]


def scatter(tab, source, own, send):
    for t, here, there in places(tab, ROWS):
        own[t] = source[here, :]
        send[t] = source[there, :]


def vector(j):
    return pl.BlockSpec((1, D), lambda *_: (0, j))


def qkv_body(first, at, tab, x_ref, p0, p1, p2, p3, gain, biases, *rest):
    step = pl.program_id(0)
    if first:
        out_ref, h_ref, w_s = rest

        @pl.when(step == 0)
        def _():
            def block(r):
                h_ref[r, :] = layer_norm(x_ref[r, :].astype(F32), gain[...], biases[:, :D]).astype(B16)

            each_block(x_ref.shape[0], 256, block)

        h = h_ref
    else:
        out_ref, w_s = rest
        h = x_ref
    assemble(tab, (p0, p1, p2, p3), w_s)
    bias = [biases[:, part * D + at : part * D + at + w_s.shape[1]] for part in (1, 2)]
    bias = jnp.where(step == 0, bias[0], jnp.where(step == 2, bias[1], 0.0))
    out_ref[0] = (mm(h[...], w_s[...], 1, 0) + bias).astype(B16)


def qkv_call(first, at, tab, x, parts, gains, biases):
    tokens = x.shape[0]
    width = parts[0].shape[2] // 3
    full = pl.BlockSpec((tokens, D), lambda j, t: (0, 0))
    piece = pl.BlockSpec((NZ, ROWS, width), lambda j, t: (0, 0, j))
    outs = [shape((3, tokens, width), B16)]
    out_specs = [pl.BlockSpec((1, tokens, width), lambda j, t: (j, 0, 0))]
    if first:
        outs.append(shape((tokens, D), B16))
        out_specs.append(full)
    return pl.pallas_call(
        functools.partial(qkv_body, first, at),
        grid_spec=pltpu.PrefetchScalarGridSpec(
            num_scalar_prefetch=1,
            grid=(3,),
            in_specs=[full, piece, piece, piece, piece, vector(0), pl.BlockSpec(biases.shape, lambda j, t: (0, 0))],
            out_specs=out_specs,
            scratch_shapes=[pltpu.VMEM((D, width), B16)],
        ),
        out_shape=outs,
        compiler_params=params(),
        cost_estimate=cost(6 * tokens * D * width, 8 * tokens * D),
        name="qkv_first" if first else "qkv_next",
    )(tab, x, *parts, gains, biases)


def each_block(count, rows, run):
    rows = min(rows, count)

    def step(b, carry):
        run(pl.ds(pl.multiple_of(b * rows, rows), rows))
        return carry

    lax.fori_loop(0, count // rows, step, 0)


def make_mask(seg_ref, mask):
    @pl.when(pl.program_id(0) == 0)
    def _():
        row = seg_ref[...].astype(F32)

        def block(r):
            mask[r, :] = jnp.where(seg_ref[:, r].astype(F32).T == row, 0.0, masked_low)

        each_block(seg_ref.shape[1], 128, block)


def attend_body(rows, q_ref, k_ref, v_ref, seg_ref, o_ref, lse_ref, mask):
    make_mask(seg_ref, mask)

    def block(r):
        for h in range(2):
            cols = slice(h * HD, (h + 1) * HD)
            q = q_ref[0, r, cols] * jnp.asarray(score_scale, B16)
            s = mm(q, k_ref[0, :, cols], 1, 1) + mask[r, :]
            top = jnp.max(s, axis=-1, keepdims=True)
            p = jnp.exp(s - top)
            total = jnp.sum(p, axis=-1, keepdims=True)
            o_ref[r, cols] = (mm(p.astype(B16), v_ref[0, :, cols], 1, 0) * (1.0 / total)).astype(B16)
            lse_ref[0, h : h + 1, r] = (top + jnp.log(total)).T

    each_block(q_ref.shape[1], rows, block)


def attend_call(qkv, seg, start=0, pairs=None):
    _, tokens, width = qkv.shape
    pairs = pairs or width // 128
    width = pairs * 128
    head = lambda j: pl.BlockSpec((1, tokens, 128), lambda i: (j, 0, i + start))
    return pl.pallas_call(
        functools.partial(attend_body, min(512, tokens)),
        grid=(pairs,),
        in_specs=[head(0), head(1), head(2), pl.BlockSpec((1, tokens), lambda i: (0, 0))],
        out_specs=[
            pl.BlockSpec((tokens, 128), lambda i: (0, i)),
            pl.BlockSpec((1, 2, tokens), lambda i: (i, 0, 0)),
        ],
        out_shape=[shape((tokens, width), B16), shape((pairs, 2, tokens), F32)],
        scratch_shapes=[pltpu.VMEM((tokens, tokens), F32)],
        compiler_params=params(),
        cost_estimate=cost(pairs * 16 * 128 * tokens * tokens, 8 * tokens * width, pairs * 2 * tokens * tokens),
        name="attend",
    )(qkv, qkv, qkv, seg)


BULK = ROWS2 + 4 * ROWS + ROWS
N16 = 16
SPARE = 16
MIDDLE_ROWS = 256


def up_body(count, *refs):
    outs, (x_ref, wo_ref, wa, wb, wc, wd, gain, biases) = refs[:count], refs[count : count + 8]
    x1_ref, h2_ref, act_ref, slope_ref, w_s = refs[count + 8 :]
    tile = w_s.shape[2]

    @pl.when(pl.program_id(0) == 0)
    def _():
        for f in range(FF // tile):
            w_s[f] = (wa, wb, wc, wd)[f // 2][:, :, (f % 2) * tile : (f % 2 + 1) * tile].reshape(D, tile)

    x1 = x_ref[...].astype(F32) + biases[:, 3 * D : 4 * D]
    wo = wo_ref[...].reshape(D, D)
    at = 0
    for o in outs:
        x1 = x1 + mm(o[...], wo[at : at + o.shape[1], :], 1, 0)
        at += o.shape[1]
    x1_ref[...] = x1
    h2_ref[...] = layer_norm(x1, gain[...], biases[:, 4 * D : 5 * D]).astype(B16)

    def pair(g, carry):
        for f in (2 * g, 2 * g + 1):
            cols = pl.ds(pl.multiple_of(f * tile, 128), tile)
            u = mm(h2_ref[...], w_s[f], 1, 0) + biases[:, pl.ds(pl.multiple_of(5 * D + f * tile, 128), tile)]
            cdf, density = normal(u)
            act_ref[:, cols] = (u * cdf).astype(B16)
            slope_ref[:, cols] = (cdf + u * density).astype(B16)
        return carry

    lax.fori_loop(0, FF // tile // 2, pair, 0)


def bulk_block(j):
    return pl.BlockSpec((N16, ROWS, D), lambda i: (0, j, 0), pipeline_mode=pl.Buffered(1))


def up_call(outs, x, bulk, gains, biases):
    tokens = x.shape[0]
    rows = min(256, tokens)
    block = lambda w: pl.BlockSpec((rows, w), lambda i: (i, 0))
    return pl.pallas_call(
        functools.partial(up_body, len(outs)),
        grid=(tokens // rows,),
        in_specs=[block(o.shape[1]) for o in outs]
        + [block(D)]
        + [bulk_block(j) for j in (8, 4, 5, 6, 7)]
        + [vector(1), pl.BlockSpec(biases.shape, lambda i: (0, 0))],
        out_specs=[block(D), block(D), block(FF), block(FF)],
        out_shape=[shape((tokens, D), F32), shape((tokens, D), B16), shape((tokens, FF), B16), shape((tokens, FF), B16)],
        scratch_shapes=[pltpu.VMEM((8, D, FF // 8), B16)],
        compiler_params=params(),
        cost_estimate=cost(2 * tokens * D * (D + FF), 30 * tokens * D, tokens * FF),
        name="up",
    )(*outs, x, bulk, bulk, bulk, bulk, bulk, gains, biases)


def down_body(act_ref, slope_ref, dy_ref, w_ref, du_ref, dw_ref, dc1, dc2):
    @pl.when(pl.program_id(0) == 0)
    def _():
        dc2[...] = jnp.sum(dy_ref[...].astype(F32), axis=0, keepdims=True)

    dc1[...] = jnp.zeros_like(dc1)

    def block(r):
        du = (mm(dy_ref[r, :], w_ref[...].reshape(D, D), 1, 1) * slope_ref[r, :].astype(F32)).astype(B16)
        du_ref[r, :] = du
        dc1[...] += jnp.sum(du.astype(F32), axis=0, keepdims=True)

    each_block(dy_ref.shape[0], 512, block)
    dw_ref[...] = mm(act_ref[...], dy_ref[...], 0, 0).astype(B16)


def down_call(act, slope, dy, bulk):
    tokens = dy.shape[0]
    ff = pl.BlockSpec((tokens, D), lambda i: (0, i))
    return pl.pallas_call(
        down_body,
        grid=(FF // D,),
        in_specs=[
            ff,
            ff,
            pl.BlockSpec((tokens, D), lambda i: (0, 0)),
            pl.BlockSpec((N16 // 4, ROWS2, D), lambda i: (i, 0, 0)),
        ],
        out_specs=[
            ff,
            pl.BlockSpec((D, D), lambda i: (i, 0)),
            vector_step(),
            pl.BlockSpec((1, D), lambda i: (0, 0)),
        ],
        out_shape=[shape((tokens, FF), B16), shape((FF, D), B16), shape((1, FF), F32), shape((1, D), F32)],
        compiler_params=params(),
        cost_estimate=cost(4 * tokens * D * FF, 30 * tokens * D),
        name="down",
    )(act, slope, dy, bulk)


def vector_step():
    return pl.BlockSpec((1, D), lambda i: (0, i))


def finish_body(act_ref, x1_ref, w_ref, c2, *refs):
    refs[-1][...] = (x1_ref[...] + c2[...] + mm(act_ref[...], w_ref[...].reshape(FF, D), 1, 0)).astype(B16)


def finish_call(act, x1, bulk, biases, start, steps, into=()):
    tokens = x1.shape[0]
    rows = tokens // 4
    block = lambda w: pl.BlockSpec((rows, w), lambda i: (i + start, 0))
    return pl.pallas_call(
        finish_body,
        grid=(steps,),
        in_specs=[
            block(FF),
            block(D),
            pl.BlockSpec((N16, ROWS2, D), lambda i: (0, 0, 0), pipeline_mode=pl.Buffered(1)),
            vector(9),
        ]
        + [pl.BlockSpec(memory_space=pl.ANY)] * len(into),
        out_specs=block(D),
        out_shape=shape((tokens, D), B16),
        input_output_aliases={4: 0} if into else {},
        compiler_params=params(),
        cost_estimate=cost(2 * steps * rows * D * FF, 20 * steps * rows * D),
        name="finish",
    )(act, x1, bulk, biases, *into)


def hidden_body(tab, h2_ref, du_ref, w_ref, acc, own, send, dw):
    @pl.when(pl.program_id(0) == 0)
    def _():
        acc[...] = jnp.zeros_like(acc)

    du = du_ref[...]
    dw[...] = mm(h2_ref[...], du, 0, 0).astype(B16)
    acc[...] += mm(du, w_ref[...].reshape(D, D), 1, 1)
    scatter(tab, dw, own, send)


def hidden_call(tab, h2, du, bulk):
    tokens = h2.shape[0]
    full = pl.BlockSpec((tokens, D), lambda i, t: (0, 0), pipeline_mode=pl.Buffered(1))
    piece = pl.BlockSpec((8, ROWS, D), lambda i, t: (0, 0, i))
    pieces = shape((8, ROWS, FF), B16)
    return pl.pallas_call(
        hidden_body,
        grid_spec=pltpu.PrefetchScalarGridSpec(
            num_scalar_prefetch=1,
            grid=(FF // D,),
            in_specs=[
                full,
                pl.BlockSpec((tokens, D), lambda i, t: (0, i)),
                pl.BlockSpec((N16, ROWS, D), lambda i, t: (0, 4 + i, 0)),
            ],
            out_specs=[pl.BlockSpec((tokens, D), lambda i, t: (0, 0)), piece, piece],
            scratch_shapes=[pltpu.VMEM((D, D), B16)],
        ),
        out_shape=[shape((tokens, D), F32), pieces, pieces],
        compiler_params=params(),
        cost_estimate=cost(4 * tokens * D * FF, 20 * tokens * D),
        name="hidden",
    )(tab, h2, du, bulk)


def middle_body(count, *refs):
    outs, (dh_ref, dy_ref, x1_ref, w_ref, gain) = refs[:count], refs[count : count + 5]
    dx_ref, do_ref, dw_ref, dvec, acc = refs[count + 5 :]
    step = pl.program_id(0)

    @pl.when(step == 0)
    def _():
        acc[...] = jnp.zeros_like(acc)
        dvec[...] = jnp.zeros_like(dvec)

    grad, dgain, dshift = layer_norm_back(x1_ref[...], gain[...], dh_ref[...])
    dx = dy_ref[...].astype(F32) + grad
    dx_ref[...] = dx
    da = dx.astype(B16)
    dvec[0:1, :] += dgain
    dvec[1:2, :] += dshift
    dvec[2:3, :] += jnp.sum(da.astype(F32), axis=0, keepdims=True)
    do_ref[...] = mm(da, w_ref[...].reshape(D, D), 1, 1).astype(B16)
    at = 0
    for o in outs:
        acc[at : at + o.shape[1], :] += mm(o[...], da, 0, 0)
        at += o.shape[1]

    @pl.when(step == pl.num_programs(0) - 1)
    def _():
        dw_ref[...] = acc[...].astype(B16)


def middle_call(outs, dh, dy, x1, bulk, gains):
    tokens = dy.shape[0]
    rows = min(MIDDLE_ROWS, tokens)
    block = lambda w: pl.BlockSpec((rows, w), lambda i: (i, 0))
    return pl.pallas_call(
        functools.partial(middle_body, len(outs)),
        grid=(tokens // rows,),
        in_specs=[block(o.shape[1]) for o in outs] + [block(D)] * 3 + [bulk_block(8), vector(1)],
        out_specs=[
            block(D),
            block(D),
            pl.BlockSpec((D, D), lambda i: (0, 0)),
            pl.BlockSpec((8, D), lambda i: (0, 0)),
        ],
        out_shape=[shape((tokens, D), F32), shape((tokens, D), B16), shape((D, D), B16), shape((8, D), F32)],
        scratch_shapes=[pltpu.VMEM((D, D), F32)],
        compiler_params=params(),
        cost_estimate=cost(4 * tokens * D * D, 20 * tokens * D),
        name="middle",
    )(*outs, dh, dy, x1, bulk, gains)


def attend_back_body(rows, q_ref, k_ref, v_ref, do_ref, o_ref, lse_ref, seg_ref, out_ref, mask, sums):
    make_mask(seg_ref, mask)
    sums[...] = jnp.zeros_like(sums)

    def block(r):
        for h in range(2):
            cols = slice(h * HD, (h + 1) * HD)
            k = k_ref[0, :, cols]
            q = q_ref[0, r, cols] * jnp.asarray(score_scale, B16)
            do = do_ref[r, cols]
            centre = jnp.sum(do.astype(F32) * o_ref[r, cols].astype(F32), axis=1, keepdims=True)
            s = mm(q, k, 1, 1) + mask[r, :]
            p = jnp.exp(s - lse_ref[0, h : h + 1, r].T)
            da = mm(do, v_ref[0, :, cols], 1, 1)
            ds = (p * (da - centre)).astype(B16)
            sums[2 * h + 1] += mm(do.T, p.astype(B16), 1, 0)
            sums[2 * h] += mm(q.T, ds, 1, 0)
            out_ref[0, r, cols] = (mm(ds, k, 1, 0) * score_scale).astype(B16)

    each_block(q_ref.shape[1], rows, block)
    for h in range(2):
        cols = slice(h * HD, (h + 1) * HD)
        out_ref[1, :, cols] = sums[2 * h].T.astype(B16)
        out_ref[2, :, cols] = sums[2 * h + 1].T.astype(B16)


def attend_back_call(qkv, do, o, lse, seg, first_pair):
    _, tokens, width = qkv.shape
    pairs = width // 128
    head = lambda j: pl.BlockSpec((1, tokens, 128), lambda i: (j, 0, i))
    return pl.pallas_call(
        functools.partial(attend_back_body, min(512, tokens)),
        grid=(pairs,),
        in_specs=[
            head(0),
            head(1),
            head(2),
            pl.BlockSpec((tokens, 128), lambda i: (0, i + first_pair)),
            pl.BlockSpec((tokens, 128), lambda i: (0, i)),
            pl.BlockSpec((1, 2, tokens), lambda i: (i, 0, 0)),
            pl.BlockSpec((1, tokens), lambda i: (0, 0)),
        ],
        out_specs=pl.BlockSpec((3, tokens, 128), lambda i: (0, 0, i)),
        out_shape=shape((3, tokens, width), B16),
        scratch_shapes=[pltpu.VMEM((tokens, tokens), F32), pltpu.VMEM((4, HD, tokens), F32)],
        compiler_params=params(),
        cost_estimate=cost(pairs * 40 * 128 * tokens * tokens, 16 * tokens * width, pairs * 2 * tokens * tokens),
        name="attend_back",
    )(qkv, qkv, qkv, do, o, lse, seg)


def weight_body(tab, h_ref, d_ref, din, dmid, dc1, dc2, own, send, dw, line, rows):
    step = pl.program_id(0)

    @pl.when(step == 0)
    def _():
        line[:, :D] = din[0:1, :]
        line[:, D : 2 * D] = dmid[0:1, :]
        for at, piece in ((2, din[1:2, :]), (3, din[2:3, :]), (4, din[3:4, :]), (5, dmid[2:3, :]), (6, dmid[1:2, :])):
            line[:, at * D : (at + 1) * D] = piece
        line[:, 7 * D : 7 * D + FF] = dc1[...]
        line[:, 7 * D + FF :] = dc2[...]
        rows[...] = jnp.zeros_like(rows)
        gains, biases = 2 * D // N16, (6 * D + FF) // N16
        for c in range(N16):
            rows[c : c + 1, :gains] = line[:, c * gains : (c + 1) * gains]
            rows[c : c + 1, gains : gains + biases] = line[:, 2 * D + c * biases : 2 * D + (c + 1) * biases]

    width = d_ref.shape[2]
    dw[...] = mm(h_ref[...], d_ref[0], 0, 0).astype(B16)
    core = tab[8]
    for t, here, there in places(tab, ROWS):
        own[t, :ROWS, :] = dw[here, :]
        send[t, :ROWS, :] = dw[there, :]
    for t in range(NZ * NX):
        base = tab[t] * 2
        for out, row in ((own, base + core), (send, base + 1 - core)):
            picked = rows[pl.ds(row, 1), pl.ds(pl.multiple_of(step * width, 128), width)]
            out[t, ROWS:, :] = jnp.broadcast_to(picked, (SPARE, width)).astype(B16)


def weight_call(tab, h1, dqkv, din, dmid, dc1, dc2):
    _, tokens, width = dqkv.shape
    piece = pl.BlockSpec((8, ROWS + SPARE, width), lambda j, t: (0, 0, j))
    pieces = shape((8, ROWS + SPARE, 3 * width), B16)
    whole = lambda v: pl.BlockSpec(v.shape, lambda j, t: (0, 0))
    return pl.pallas_call(
        weight_body,
        grid_spec=pltpu.PrefetchScalarGridSpec(
            num_scalar_prefetch=1,
            grid=(3,),
            in_specs=[
                pl.BlockSpec((tokens, D), lambda j, t: (0, 0)),
                pl.BlockSpec((1, tokens, width), lambda j, t: (j, 0, 0)),
            ]
            + [whole(v) for v in (din, dmid, dc1, dc2)],
            out_specs=[piece, piece],
            scratch_shapes=[
                pltpu.VMEM((D, width), B16),
                pltpu.VMEM((1, 8 * D + FF), F32),
                pltpu.VMEM((N16, 3 * width), F32),
            ],
        ),
        out_shape=[pieces, pieces],
        compiler_params=params(),
        cost_estimate=cost(6 * tokens * D * width, 12 * tokens * width),
        name="qkv_weight",
    )(tab, h1, dqkv, din, dmid, dc1, dc2)


def joint_body(h_ref, d_ref, o_ref, dw):
    width = d_ref.shape[2]
    dw[:, :width] = mm(h_ref[...], d_ref[0], 0, 0).astype(B16)
    dw[:, width:] = o_ref[...]


def joint_call(h1, dqkv, dwo):
    _, tokens, width = dqkv.shape
    side = D // 3
    return pl.pallas_call(
        joint_body,
        grid=(3,),
        in_specs=[
            pl.BlockSpec((tokens, D), lambda j: (0, 0)),
            pl.BlockSpec((1, tokens, width), lambda j: (j, 0, 0)),
            pl.BlockSpec((D, side), lambda j: (0, j)),
        ],
        out_specs=pl.BlockSpec((D, width + side), lambda j: (0, j)),
        out_shape=shape((D, 3 * (width + side)), B16),
        compiler_params=params(),
        cost_estimate=cost(6 * tokens * D * width, 12 * tokens * width),
        name="joint_weight",
    )(h1, dqkv, dwo)


def split_joint(total):
    side = D // 3
    parts = jnp.split(total, 3, axis=1)
    width = parts[0].shape[1] - side
    return jnp.concatenate([p[:, :width] for p in parts], axis=1), jnp.concatenate([p[:, width:] for p in parts], axis=1)


def input_body(tab, da_ref, db_ref, x_ref, dx_ref, a0, a1, a2, a3, b0, b1, b2, b3, gain, *refs):
    out_ref, dvec, wa, wb = refs[-4:]
    step = pl.program_id(0)

    @pl.when(step == 0)
    def _():
        assemble(tab, (a0, a1, a2, a3), wa)
        assemble(tab, (b0, b1, b2, b3), wb)
        dvec[...] = jnp.zeros_like(dvec)

    dh, at = None, 0
    for d_ref, w in ((da_ref, wa), (db_ref, wb)):
        width = d_ref.shape[2]
        for j in range(3):
            term = mm(d_ref[j], w[:, j * width : (j + 1) * width], 1, 1)
            dh = term if dh is None else dh + term
        for j, row in ((0, 2), (2, 3)):
            dvec[row : row + 1, at : at + width] += jnp.sum(d_ref[j].astype(F32), axis=0, keepdims=True)
        at += width
    grad, dgain, dshift = layer_norm_back(x_ref[...].astype(F32), gain[...], dh)
    out_ref[...] = dx_ref[...] + grad
    dvec[0:1, :] += dgain
    dvec[1:2, :] += dshift


def input_call(tab, da, db, x, dx, parts_a, parts_b, gain):
    tokens = x.shape[0]
    rows = tokens // 4
    wa, wb = da.shape[2], db.shape[2]
    grads = lambda w: pl.BlockSpec((3, rows, w), lambda i, t: (0, i, 0))
    block = pl.BlockSpec((rows, D), lambda i, t: (i, 0))
    piece = lambda w: pl.BlockSpec((NZ, ROWS, 3 * w), lambda i, t: (0, 0, 0), pipeline_mode=pl.Buffered(1))
    return pl.pallas_call(
        input_body,
        grid_spec=pltpu.PrefetchScalarGridSpec(
            num_scalar_prefetch=1,
            grid=(4,),
            in_specs=[grads(wa), grads(wb), block, block]
            + [piece(wa)] * 4
            + [piece(wb)] * 4
            + [vector(0)],
            out_specs=[block, pl.BlockSpec((8, D), lambda i, t: (0, 0))],
            scratch_shapes=[pltpu.VMEM((D, 3 * wa), B16), pltpu.VMEM((D, 3 * wb), B16)],
        ),
        out_shape=[shape((tokens, D), F32), shape((8, D), F32)],
        compiler_params=params(),
        cost_estimate=cost(6 * tokens * D * D, 20 * tokens * D),
        name="input_grad",
    )(tab, da, db, x, dx, *parts_a, *parts_b, gain)


def small_params():
    return pltpu.CompilerParams(vmem_limit_bytes=40 * 1024 * 1024)


def add(a, b):
    return a + b


def stack_body(*refs):
    for i, ref in enumerate(refs[:-1]):
        refs[-1][i] = ref[...]


def stack(parts):
    return pl.pallas_call(
        stack_body,
        out_shape=shape((len(parts), *parts[0].shape), parts[0].dtype),
        compiler_params=small_params(),
        cost_estimate=cost(0, 16 * parts[0].size),
        name="stack",
    )(*parts)


def split_body(grid, a, b, keep, send):
    if grid:
        keep[0] = add(a[0, 0], b[0, 0])
        send[0] = add(a[1, 0], b[1, 0])
    else:
        keep[...] = add(a[0], b[0])
        send[...] = add(a[1], b[1])


def add_split(own, received, grid=True):
    _, r, w = own.shape
    both = pl.BlockSpec((NX, 1, r, w), lambda i: (0, i, 0, 0))
    one = pl.BlockSpec((1, r, w), lambda i: (i, 0, 0))
    how = dict(grid=(NZ,), in_specs=[both, both], out_specs=[one, one], compiler_params=params())
    return pl.pallas_call(
        functools.partial(split_body, grid),
        out_shape=[shape((NZ, r, w), B16)] * 2,
        cost_estimate=cost(8 * r * w, 48 * r * w),
        name="add_split",
        **(how if grid else dict(compiler_params=small_params())),
    )(own.reshape(NX, NZ, r, w), received.reshape(NX, NZ, r, w))


def halves_body(tab, a0, b0, a1, b1, keep, send):
    keep[...] = add(a0[...], b0[...])
    send[...] = add(a1[...], b1[...])


def add_halves(tab, own, received):
    n, r, w = own.shape
    mine = pl.BlockSpec((2, r, w // 2), lambda i, t: (i, 0, t[9]))
    other = pl.BlockSpec((2, r, w // 2), lambda i, t: (i, 0, 1 - t[9]))
    one = pl.BlockSpec((2, r, w // 2), lambda i, t: (i, 0, 0))
    return pl.pallas_call(
        halves_body,
        grid_spec=pltpu.PrefetchScalarGridSpec(
            num_scalar_prefetch=1, grid=(n // 2,), in_specs=[mine, mine, other, other], out_specs=[one, one]
        ),
        out_shape=[shape((n, r, w // 2), B16)] * 2,
        compiler_params=params(),
        cost_estimate=cost(8 * r * w, 48 * r * w),
        name="add_halves",
    )(tab, own, received, own, received)


def vectors_body(tab, p0, p1, p2, p3, gains, biases, rows):
    parts = (p0, p1, p2, p3)
    core = tab[8]
    for t in range(NZ * NX):
        rx, rz = divmod(t, NZ)
        base = tab[t] * 2
        rows[pl.ds(base + core, 1), :] = parts[rx][rz, 0:1, :].astype(F32)
        rows[pl.ds(base + 1 - core, 1), :] = parts[2 + rx][rz, 0:1, :].astype(F32)
    at = 0
    for out in (gains, biases):
        n = out.shape[1] // N16
        for c in range(N16):
            out[:, c * n : (c + 1) * n] = rows[c : c + 1, at : at + n]
        at += n


def read_vectors(tab, parts, ngain, nbias):
    width = parts[0].shape[2]
    part = pl.BlockSpec((NZ, SPARE, width), lambda i, t: (0, ROWS // SPARE, 0))
    whole = lambda n: pl.BlockSpec((1, N16 * n), lambda i, t: (0, 0))
    return pl.pallas_call(
        vectors_body,
        grid_spec=pltpu.PrefetchScalarGridSpec(
            num_scalar_prefetch=1,
            grid=(1,),
            in_specs=[part] * 4,
            out_specs=[whole(ngain), whole(nbias)],
            scratch_shapes=[pltpu.VMEM((N16, width), F32)],
        ),
        out_shape=[shape((1, N16 * ngain), F32), shape((1, N16 * nbias), F32)],
        name="vectors",
    )(tab, *parts)


def parts_body(a, b, *outs):
    for i, out in enumerate(outs):
        out[...] = add(a[i], b[i])


def add_parts(keep, received):
    n, r, w = keep.shape
    return pl.pallas_call(
        parts_body,
        out_shape=[shape((r, w), B16)] * n,
        compiler_params=small_params(),
        cost_estimate=cost(4 * r * w, 24 * r * w),
        name="add_parts",
    )(keep, received)


def four_body(a, b, c, d, out):
    out[...] = ((a[...].astype(F32) + b[...].astype(F32)) + (c[...].astype(F32) + d[...].astype(F32))).astype(B16)


def add_four(parts):
    return pl.pallas_call(
        four_body,
        out_shape=shape(parts[0].shape, B16),
        compiler_params=small_params(),
        cost_estimate=cost(4 * parts[0].size, 10 * parts[0].size),
        name="add_four",
    )(*parts)


def tie(*trees):
    flat, tree = jax.tree.flatten(trees)
    return jax.tree.unflatten(tree, lax.optimization_barrier(flat))


def flip(value, axis, size, by):
    return lax.ppermute(value, axis, [(i, i ^ by) for i in range(size)])


def along_z(value):
    return [flip(value, "z", NZ, by) for by in range(1, NZ)]


def swap_z(parts):
    return [flip(parts[by], "z", NZ, by) for by in range(1, NZ)]


def along_x(value):
    return flip(value, "x", NX, 1)


def across(value):
    return flip(value, "core", 2, 1)


def along_rep(value):
    return flip(value, "rep", 2, 1)


def bounds_of():
    out, at = [], 0
    for heads in FWD_GROUPS:
        out.append((at * HD, (at + heads) * HD))
        at += heads
    return out


def qkv_shards(w_qkv):
    shard = w_qkv.reshape(-1, 3 * D)
    return [jnp.concatenate([shard[:, part * D + a : part * D + b] for part in range(3)], axis=1) for a, b in bounds_of()]


def column_blocks(w):
    return [w[:, j * D : (j + 1) * D] for j in range(w.shape[1] // D)]


def gather_vectors(gains, biases):
    count = 1
    for axis in FSDP:
        count *= lax.axis_size(axis)
    vec = jnp.concatenate([gains, biases])
    vec = lax.all_to_all(
        jnp.broadcast_to(vec[None], (count, vec.shape[0])), FSDP, split_axis=0, concat_axis=0, tiled=True
    ).astype(F32)
    n = gains.shape[0]
    return vec[:, :n].reshape(1, -1), vec[:, n:].reshape(1, -1)


def reduce_small(dgains, dbiases):
    count, reps = 1, lax.axis_size("rep")
    for axis in FSDP:
        count *= lax.axis_size(axis)
    small = jnp.concatenate([dgains.reshape(count, -1), dbiases.reshape(count, -1)], axis=1)
    small = jnp.broadcast_to(small[:, None], (count, reps, small.shape[1])).reshape(count * reps, -1)
    small = lax.all_to_all(small, FSDP + ("rep",), split_axis=0, concat_axis=0, tiled=True)
    small = jnp.sum(small, axis=0)
    n = dgains.shape[0] // count
    return small[:n], small[n:]


def small_gradients(din, dmid, dc1, dc2):
    dgains = jnp.concatenate([din[0], dmid[0]])
    dbiases = jnp.concatenate([din[1], din[2], din[3], dmid[2], dmid[1], dc1[0], dc2[0]])
    return dgains, dbiases


def join_qkv(grads):
    widths = [b - a for a, b in bounds_of()]
    return jnp.concatenate(
        [g[:, part * w : (part + 1) * w] for part in range(3) for g, w in zip(grads, widths)], axis=1
    ).reshape(-1)


def shards(tokens, w_qkv, w_out, w_fc1, w_fc2, gains, biases, segment, cotangent):
    mz, mx, core = lax.axis_index("z"), lax.axis_index("x"), lax.axis_index("core")
    rep = lax.axis_index("rep")
    tab = jnp.stack(
        [((mz ^ rz) * NX + (mx ^ rx)).astype(jnp.int32) for rx in range(NX) for rz in range(NZ)]
        + [core.astype(jnp.int32), rep.astype(jnp.int32)]
    )
    seg = segment.reshape(1, -1)
    pairs = [(b - a) // 128 for a, b in bounds_of()]
    starts = [a for a, _ in bounds_of()]
    s0, s1 = qkv_shards(w_qkv)
    vec = jnp.concatenate([gains, biases]).reshape(1, -1)
    s0 = jnp.concatenate([s0, jnp.pad(vec, ((0, SPARE - 1), (0, s0.shape[1] - vec.shape[1])))])
    bulk = jnp.concatenate([w_fc2.reshape(ROWS2, D), *column_blocks(w_fc1.reshape(ROWS, FF)), w_out.reshape(ROWS, D)])
    bulk = lax.dynamic_slice_in_dim(bulk, rep * (BULK // 2), BULK // 2)
    bulk = lax.all_gather(bulk, FSDP + ("rep",), axis=0, tiled=False).reshape(N16, BULK, D)

    z0 = along_z(s0)
    z0, s1 = tie(z0, s1)
    a0 = stack([s0, *z0])
    x0, c0 = along_x(a0), across(a0)
    z1 = along_z(s1)
    x0, c0 = tie(x0, c0)
    w0 = (a0, x0, c0, across(x0))
    gain_all, bias_all = read_vectors(tab, w0, gains.shape[0], biases.shape[0])
    qkv0, h1 = qkv_call(True, starts[0], tab, tokens, w0, gain_all, bias_all)
    qkv0, z1 = tie(qkv0, z1)
    a1 = stack([s1, *z1])
    x1, c1 = along_x(a1), across(a1)
    o0, lse0 = attend_call(qkv0, seg)
    o0, x1, c1, h1 = tie(o0, x1, c1, h1)
    w1 = (a1, x1, c1, across(x1))
    (qkv1,) = qkv_call(False, starts[1], tab, h1, w1, gain_all, bias_all)
    o1, lse1 = attend_call(qkv1, seg)
    outs = [o0, o1]
    x1, h2, act, slope = up_call(outs, tokens, bulk, gain_all, bias_all)

    du, dw2, dc1, dc2 = down_call(act, slope, cotangent, bulk)
    r2 = lax.psum_scatter(dw2, FSDP, scatter_dimension=0, tiled=True)
    dh, own1, send1 = hidden_call(tab, h2, du, bulk)
    r1 = across(send1)
    dx1, do, dwo, dmid = middle_call(outs, dh, cotangent, x1, bulk, gain_all)
    do, r1 = tie(do, r1)
    keep, give = add_halves(tab, own1, r1)
    do, give = tie(do, give)
    r1 = along_rep(give)
    d1 = attend_back_call(qkv1, do, o1, lse1, seg, pairs[0])
    d1, r1 = tie(d1, r1)
    dwq = joint_call(h1, d1, dwo)
    rq = lax.psum_scatter(dwq, FSDP, scatter_dimension=0, tiled=True)
    keep, give = add_split(keep, r1)
    dwq, give, do = tie(dwq, give, do)
    r1 = along_x(give)
    d0 = attend_back_call(qkv0, do, o0, lse0, seg, 0)
    d0, r1 = tie(d0, r1)
    parts1 = add_parts(keep, r1)
    parts1, d0 = tie(parts1, d0)
    r1 = swap_z(parts1)
    grad_tokens, din = input_call(tab, d0, d1, tokens, dx1, w0, w1, gain_all)
    din, r1, r2 = tie(din, r1, r2)
    total1 = add_four([parts1[0], *r1])
    total1, din, r2 = tie(total1, din, r2)
    y1, y2 = along_rep(total1), along_rep(r2)
    own_p, send_p = weight_call(tab, h1, d0, din, dmid, dc1, dc2)
    send_p, y1, y2 = tie(send_p, y1, y2)
    rp = across(send_p)
    keepp, givep = add_split(own_p, rp, False)
    givep, act = tie(givep, act)
    rp = along_x(givep)
    output = finish_call(act, x1, bulk, bias_all, 0, 2)
    output, rp = tie(output, rp)
    partsp = add_parts(keepp, rp)
    partsp, output = tie(partsp, output)
    rp = swap_z(partsp)
    output = finish_call(act, x1, bulk, bias_all, 2, 2, (output,))
    output, rp, rq = tie(output, rp, rq)
    totalp = add_four([partsp[0], *rp])
    yp, yq = along_rep(totalp), along_rep(rq)
    gradp = totalp.astype(F32) + yp.astype(F32)
    small = gradp[ROWS, : gains.shape[0] + biases.shape[0]]
    gradq, grado = split_joint(rq.astype(F32) + yq.astype(F32))
    grad1 = jnp.where(rep == 0, jnp.concatenate([total1, y1], axis=1), jnp.concatenate([y1, total1], axis=1))
    return (
        output,
        grad_tokens,
        join_qkv([gradp[:ROWS], gradq]),
        grado.reshape(-1),
        grad1.astype(F32).reshape(-1),
        (r2.astype(F32) + y2.astype(F32)).reshape(-1),
        small[: gains.shape[0]],
        small[gains.shape[0] :],
    )


def gather_any(shard):
    whole = lax.all_gather(shard, FSDP, axis=0, tiled=True)
    blocks = whole.reshape(NZ, NX, 2, -1, whole.shape[1]).transpose(2, 1, 0, 3, 4)
    return blocks[0, 0], blocks[0, 1], blocks[1, 0], blocks[1, 1]


def sum_rows(whole):
    part = lax.psum_scatter(whole, FSDP, scatter_dimension=0, tiled=True)
    return lax.psum(part, "rep").astype(F32)


def reduce_any(own, send):
    blocks = jnp.stack([own, send]).reshape(2, NX, NZ, *own.shape[1:]).transpose(2, 1, 0, 3, 4)
    return sum_rows(blocks.reshape(-1, own.shape[2]))


def shards_any(tokens, w_qkv, w_out, w_fc1, w_fc2, gains, biases, segment, cotangent):
    tab = jnp.asarray([rz * NX + rx for rx in range(NX) for rz in range(NZ)] + [0], jnp.int32)
    seg = segment.reshape(1, -1)
    pairs = [(b - a) // 128 for a, b in bounds_of()]
    w0, w1 = [gather_any(s) for s in qkv_shards(w_qkv)]
    lower, wide, out = [
        lax.all_gather(w.reshape(-1, n), FSDP, axis=0, tiled=True) for w, n in ((w_fc2, D), (w_fc1, FF), (w_out, D))
    ]
    bulk = jnp.concatenate([b.reshape(N16, -1, D) for b in (lower, *column_blocks(wide), out)], axis=1)
    gain_all, bias_all = gather_vectors(gains, biases)
    starts = [a for a, _ in bounds_of()]
    qkv0, h1 = qkv_call(True, starts[0], tab, tokens, w0, gain_all, bias_all)
    (qkv1,) = qkv_call(False, starts[1], tab, h1, w1, gain_all, bias_all)
    o0, lse0 = attend_call(qkv0, seg)
    o1, lse1 = attend_call(qkv1, seg)
    outs = [o0, o1]
    x1, h2, act, slope = up_call(outs, tokens, bulk, gain_all, bias_all)
    output = finish_call(act, x1, bulk, bias_all, 0, 4)
    du, dw2, dc1, dc2 = down_call(act, slope, cotangent, bulk)
    dh, own1, send1 = hidden_call(tab, h2, du, bulk)
    dx1, do, dwo, dmid = middle_call(outs, dh, cotangent, x1, bulk, gain_all)
    d1 = attend_back_call(qkv1, do, o1, lse1, seg, pairs[0])
    d0 = attend_back_call(qkv0, do, o0, lse0, seg, 0)
    dwq = joint_call(h1, d1, dwo)
    grad_tokens, din = input_call(tab, d0, d1, tokens, dx1, w0, w1, gain_all)
    own_p, send_p = [v[:, :ROWS] for v in weight_call(tab, h1, d0, din, dmid, dc1, dc2)]
    gradq, grado = split_joint(sum_rows(dwq))
    return (
        output,
        grad_tokens,
        join_qkv([reduce_any(own_p, send_p), gradq]),
        grado.reshape(-1),
        reduce_any(own1, send1).reshape(-1),
        sum_rows(dw2).reshape(-1),
        *reduce_small(*small_gradients(din, dmid, dc1, dc2)),
    )


def solution(mesh):
    count, reps = mesh.shape["fsdp"], mesh.shape["rep"]
    inner = Mesh(mesh.devices.reshape(count // 4, 2, 2, reps), FSDP + ("rep",))
    rows = P(FSDP + ("rep",), None)
    flat = P(FSDP)
    return jax.shard_map(
        shards if (count, reps) == (2 * NZ * NX, 2) else shards_any,
        mesh=inner,
        in_specs=(rows, flat, flat, flat, flat, flat, flat, P(FSDP + ("rep",)), rows),
        out_specs=(rows, rows, flat, flat, flat, flat, flat, flat),
        check_vma=False,
    )
```

profile of v0, /device:TPU:16, one launch (start us, length us, event | category | flops | bytes accessed | tf_op | source)
XLA Modules:
  0.0 325.4 jit_solution(17720000370383833111)
XLA Ops:
  7.2 1.0 reshape.72
  8.3 1.1 reshape.71
  9.4 1.2 reshape.70
  10.7 0.8 constant_dynamic-slice_fusion
  12.0 0.5 collective-permute-start.2
  12.5 3.5 %collective-permute-start.1 = (bf16[64,768]{1,0:T(8,128)(2,1)S(1)}, bf16[64,768]{1,0:T(8,128)(2,1)S(1)}, u32[]{:S(2)}, u32[]{:S(2)}) collective-permute-start(bf16[64,768]{1,0:T(8,128)(2,1)S(1)} %fusion.1.refs_0_), channel_id=1, source_target_pairs={{0,16},{8,24},{16,0},{24,8},{1,17},{9,25},{17,1},{25,9},{2,18},{10... | collective-permute-start | bytes 294920 | tf_op jit(solution)/shard_map/ppermute | solution.py:762
  16.0 5.9 %collective-permute-done.2.refs_3_ = bf16[64,768]{1,0:T(8,128)(2,1)S(1)} collective-permute-done((bf16[64,768]{1,0:T(8,128)(2,1)S(1)}, bf16[64,768]{1,0:T(8,128)(2,1)S(1)}, u32[]{:S(2)}, u32[]{:S(2)}) %collective-permute-start.2) | collective-permute-done | bytes 98336 | tf_op jit(solution)/shard_map/ppermute | solution.py:762
  22.0 1.6 collective-permute-start.3
  23.7 11.1 %collective-permute-done.3.p1.a1 = bf16[4,64,768]{2,1,0:T(8,128)(2,1)S(1)} collective-permute-done((bf16[4,64,768]{2,1,0:T(8,128)(2,1)S(1)}, bf16[4,64,768]{2,1,0:T(8,128)(2,1)S(1)}, u32[]{:S(2)}, u32[]{:S(2)}) %collective-permute-start.3) | collective-permute-done | bytes 393248 | tf_op jit(solution)/shard_map/ppermute | solution.py:762
  34.8 0.6 collective-permute-start.8
  35.4 3.3 %collective-permute-start.7 = (bf16[48,1536]{1,0:T(8,128)(2,1)S(1)}, bf16[48,1536]{1,0:T(8,128)(2,1)S(1)}, u32[]{:S(2)}, u32[]{:S(2)}) collective-permute-start(bf16[48,1536]{1,0:T(8,128)(2,1)S(1)} %pad_maximum_fusion.refs_0_), channel_id=1, source_target_pairs={{0,16},{8,24},{16,0},{24,8},{1,17},{9,25},{17,1},{25,9},{2,18},{10... | collective-permute-start | bytes 442376 | tf_op jit(solution)/shard_map/ppermute | solution.py:762
  38.7 0.7 stack.45.tab
  39.4 0.7 copy-done.8
  40.1 2.5 vectors.1
  42.6 6.9 %qkv_first.1 = (bf16[3,1024,256]{2,1,0:T(8,128)(2,1)}, bf16[1024,768]{1,0:T(8,128)(2,1)}) custom-call(s32[10]{0:T(128)} %stack.45.tab, bf16[1024,768]{1,0:T(8,128)(2,1)} %x_ref.3, bf16[4,64,768]{2,1,0:T(8,128)(2,1)} %copy-done, bf16[4,64,768]{2,1,0:T(8,128)(2,1)} %copy-done.7, bf16[4,64,768]{2,1,0:T(8,128)(2,1)} %copy-done.6, bf16[4,64,768]{2,1,0:T(8,128)(2,1)} %copy-done.8, ...), custom_call_target="tpu_custom_call" | custom-call | flops 1207959552 | bytes 6291456 | tf_op jit(solution)/shard_map/qkv_first/pallas_call | solution.py:137
  49.5 3.1 collective-permute-done.8.refs_3_
  52.6 7.0 %collective-permute-done.7.refs_2_ = bf16[48,1536]{1,0:T(8,128)(2,1)S(1)} collective-permute-done((bf16[48,1536]{1,0:T(8,128)(2,1)S(1)}, bf16[48,1536]{1,0:T(8,128)(2,1)S(1)}, u32[]{:S(2)}, u32[]{:S(2)}) %collective-permute-start.7) | collective-permute-done | bytes 147488 | tf_op jit(solution)/shard_map/ppermute | solution.py:762
  60.0 12.4 %attend.2 = (bf16[1024,256]{1,0:T(8,128)(2,1)}, f32[2,2,1024]{2,1,0:T(2,128)}) custom-call(bf16[3,1024,256]{2,1,0:T(8,128)(2,1)} %get-tuple-element.112.q_ref.k_ref.v_ref, bf16[3,1024,256]{2,1,0:T(8,128)(2,1)} %get-tuple-element.112.q_ref.k_ref.v_ref, bf16[3,1024,256]{2,1,0:T(8,128)(2,1)} %get-tuple-element.112.q_ref.k_ref.v_ref, s32[1,1024]{1,0:T(1,128)} %bitcast.38), custom_call_target="tpu_custom_call" | custom-call | flops 4294967296 | bytes 2097152 | tf_op jit(solution)/shard_map/attend/pallas_call | solution.py:196
  72.4 6.1 %collective-permute-done.9.p1.b1 = bf16[4,48,1536]{2,1,0:T(8,128)(2,1)S(1)} collective-permute-done((bf16[4,48,1536]{2,1,0:T(8,128)(2,1)S(1)}, bf16[4,48,1536]{2,1,0:T(8,128)(2,1)S(1)}, u32[]{:S(2)}, u32[]{:S(2)}) %collective-permute-start.9) | collective-permute-done | bytes 589856 | tf_op jit(solution)/shard_map/ppermute | solution.py:762
  78.5 2.0 collective-permute-done.11.p3.b3
  80.5 0.9 copy-done.16
  81.4 7.2 %qkv_next.1.q_ref.k_ref.v_ref = bf16[3,1024,512]{2,1,0:T(8,128)(2,1)} custom-call(s32[10]{0:T(128)} %stack.45.tab, bf16[1024,768]{1,0:T(8,128)(2,1)} %get-tuple-element.118.x_ref.h_ref, bf16[4,48,1536]{2,1,0:T(8,128)(2,1)} %copy-done.2, bf16[4,48,1536]{2,1,0:T(8,128)(2,1)} %copy-done.15, bf16[4,48,1536]{2,1,0:T(8,128)(2,1)} %copy-done.14, ...), custom_call_target="tpu_custom_call" | custom-call | flops 2415919104 | bytes 6291456 | tf_op jit(solution)/shard_map/qkv_next/pallas_call | solution.py:137
  88.7 21.6 %attend.3 = (bf16[1024,512]{1,0:T(8,128)(2,1)}, f32[4,2,1024]{2,1,0:T(2,128)}) custom-call(bf16[3,1024,512]{2,1,0:T(8,128)(2,1)} %qkv_next.1.q_ref.k_ref.v_ref, bf16[3,1024,512]{2,1,0:T(8,128)(2,1)} %qkv_next.1.q_ref.k_ref.v_ref, bf16[3,1024,512]{2,1,0:T(8,128)(2,1)} %qkv_next.1.q_ref.k_ref.v_ref, s32[1,1024]{1,0:T(1,128)} %bitcast.39), custom_call_target="tpu_custom_call" | custom-call | flops 8589934592 | bytes 4194304 | tf_op jit(solution)/shard_map/attend/pallas_call | solution.py:196
  110.3 1.0 all-gather.3.cloned.1.call-done
  111.3 25.4 %up.1 = (f32[1024,768]{1,0:T(8,128)}, bf16[1024,768]{1,0:T(8,128)(2,1)}, bf16[1024,3072]{1,0:T(8,128)(2,1)}, bf16[1024,3072]{1,0:T(8,128)(2,1)}) custom-call(bf16[1024,256]{1,0:T(8,128)(2,1)} %get-tuple-element.119.refs_0_.o_ref, bf16[1024,512]{1,0:T(8,128)(2,1)} %get-tuple-element.122.refs_1_.o_ref, bf16[1024,768]{1,0:T(8,128)(2,1)} %x_ref.3, ...), custom_call_target="tpu_custom_call" | custom-call | flops 6039797760 | bytes 23592960 | tf_op jit(solution)/shard_map/up/pallas_call | solution.py:257
  136.7 16.8 %down.1 = (bf16[1024,3072]{1,0:T(8,128)(2,1)}, bf16[3072,768]{1,0:T(8,128)(2,1)}, f32[1,3072]{1,0:T(1,128)}, f32[1,768]{1,0:T(1,128)}) custom-call(bf16[1024,3072]{1,0:T(8,128)(2,1)} %get-tuple-element.176.act_ref, bf16[1024,3072]{1,0:T(8,128)(2,1)} %get-tuple-element.125.slope_ref, bf16[1024,768]{1,0:T(8,128)(2,1)} %refs_3_.1, bf16[16,432,768]{2,1,0:T(8,128)(2,1)} %bitcast.29), custom_call_target="tpu_custom_call" | custom-call | flops 9663676416 | bytes 23592960 | tf_op jit(solution)/shard_map/down/pallas_call | solution.py:292
  153.6 16.1 %hidden.1 = (f32[1024,768]{1,0:T(8,128)}, bf16[8,48,3072]{2,1,0:T(8,128)(2,1)}, bf16[8,48,3072]{2,1,0:T(8,128)(2,1)}) custom-call(s32[10]{0:T(128)} %stack.45.tab, bf16[1024,768]{1,0:T(8,128)(2,1)} %get-tuple-element.123.h2_ref, bf16[1024,3072]{1,0:T(8,128)(2,1)} %get-tuple-element.126.du_ref, bf16[16,432,768]{2,1,0:T(8,128)(2,1)} %bitcast.30), custom_call_target="tpu_custom_call" | custom-call | flops 9663676416 | bytes 15728640 | tf_op jit(solution)/shard_map/hidden/pallas_call | solution.py:361
  169.9 10.3 %middle.1 = (f32[1024,768]{1,0:T(8,128)}, bf16[1024,768]{1,0:T(8,128)(2,1)}, bf16[768,768]{1,0:T(8,128)(2,1)}, f32[8,768]{1,0:T(8,128)}) custom-call(bf16[1024,256]{1,0:T(8,128)(2,1)} %get-tuple-element.119.refs_0_.o_ref, bf16[1024,512]{1,0:T(8,128)(2,1)} %get-tuple-element.122.refs_1_.o_ref, f32[1024,768]{1,0:T(8,128)} %get-tuple-element.128.refs_2_, ...), custom_call_target="tpu_custom_call" | custom-call | flops 2415919104 | bytes 15728640 | tf_op jit(solution)/shard_map/middle/pallas_call | solution.py:413
  180.2 1.4 copy-done.4
  181.6 5.0 %add_halves.1 = (bf16[8,48,1536]{2,1,0:T(8,128)(2,1)}, bf16[8,48,1536]{2,1,0:T(8,128)(2,1)}) custom-call(s32[10]{0:T(128)} %stack.45.tab, bf16[8,48,3072]{2,1,0:T(8,128)(2,1)} %get-tuple-element.127.a0.a1, bf16[8,48,3072]{2,1,0:T(8,128)(2,1)} %copy-done.4, bf16[8,48,3072]{2,1,0:T(8,128)(2,1)} %get-tuple-element.127.a0.a1, bf16[8,48,3072]{2,1,0:T(8,128)(2,1)} %copy-done.4), custom_call_target="tpu_custom_call" | custom-call | flops 1179648 | bytes 7077888 | tf_op jit(solution)/shard_map/add_halves/pallas_call | solution.py:680
  186.6 1.5 collective-permute-start.13
  188.0 29.4 %attend_back.2.d_ref.db_ref = bf16[3,1024,512]{2,1,0:T(8,128)(2,1)} custom-call(bf16[3,1024,512]{2,1,0:T(8,128)(2,1)} %qkv_next.1.q_ref.k_ref.v_ref, bf16[3,1024,512]{2,1,0:T(8,128)(2,1)} %qkv_next.1.q_ref.k_ref.v_ref, bf16[3,1024,512]{2,1,0:T(8,128)(2,1)} %qkv_next.1.q_ref.k_ref.v_ref, bf16[1024,768]{1,0:T(8,128)(2,1)} %get-tuple-element.144.do_ref, ...), custom_call_target="tpu_custom_call" | custom-call | flops 21474836480 | bytes 8388608 | tf_op jit(solution)/shard_map/attend_back/pallas_call | solution.py:461
  217.5 7.6 %joint_weight.1 = bf16[768,2304]{1,0:T(8,128)(2,1)} custom-call(bf16[1024,768]{1,0:T(8,128)(2,1)} %get-tuple-element.118.x_ref.h_ref, bf16[3,1024,512]{2,1,0:T(8,128)(2,1)} %attend_back.2.d_ref.db_ref, bf16[768,768]{1,0:T(8,128)(2,1)} %get-tuple-element.142.o_ref), custom_call_target="tpu_custom_call" | custom-call | flops 2415919104 | bytes 6291456 | tf_op jit(solution)/shard_map/joint_weight/pallas_call | solution.py:550
  225.0 3.7 %add_split.2 = (bf16[4,48,1536]{2,1,0:T(8,128)(2,1)}, bf16[4,48,1536]{2,1,0:T(8,128)(2,1)}) custom-call(bf16[2,4,48,1536]{3,2,1,0:T(8,128)(2,1)} %bitcast.34, bf16[2,4,48,1536]{3,2,1,0:T(8,128)(2,1)} %bitcast.35), custom_call_target="tpu_custom_call" | custom-call | flops 589824 | bytes 3538944 | tf_op jit(solution)/shard_map/add_split/pallas_call | solution.py:661
  228.7 0.9 collective-permute-start.14
  229.6 16.5 %attend_back.3.da_ref.d_ref = bf16[3,1024,256]{2,1,0:T(8,128)(2,1)} custom-call(bf16[3,1024,256]{2,1,0:T(8,128)(2,1)} %get-tuple-element.112.q_ref.k_ref.v_ref, bf16[3,1024,256]{2,1,0:T(8,128)(2,1)} %get-tuple-element.112.q_ref.k_ref.v_ref, bf16[3,1024,256]{2,1,0:T(8,128)(2,1)} %get-tuple-element.112.q_ref.k_ref.v_ref, ...), custom_call_target="tpu_custom_call" | custom-call | flops 10737418240 | bytes 4194304 | tf_op jit(solution)/shard_map/attend_back/pallas_call | solution.py:461
  246.2 4.4 %collective-permute-start.15 = (bf16[48,1536]{1,0:T(8,128)(2,1)S(1)}, bf16[48,1536]{1,0:T(8,128)(2,1)S(1)}, u32[]{:S(2)}, u32[]{:S(2)}) collective-permute-start(bf16[48,1536]{1,0:T(8,128)(2,1)S(1)} %get-tuple-element.157), channel_id=1, source_target_pairs={{0,8},{8,0},{16,24},{24,16},{1,9},{9,1},{17,25},{25,17},{2,10},{10... | collective-permute-start | bytes 442376 | tf_op jit(solution)/shard_map/ppermute | solution.py:762
  250.5 1.7 collective-permute-start.16
  252.2 0.5 collective-permute-start.17
  252.7 11.1 %input_grad.1 = (f32[1024,768]{1,0:T(8,128)}, f32[8,768]{1,0:T(8,128)}) custom-call(s32[10]{0:T(128)} %stack.45.tab, bf16[3,1024,256]{2,1,0:T(8,128)(2,1)} %attend_back.3.da_ref.d_ref, bf16[3,1024,512]{2,1,0:T(8,128)(2,1)} %attend_back.2.d_ref.db_ref, bf16[1024,768]{1,0:T(8,128)(2,1)} %x_ref.3, f32[1024,768]{1,0:T(8,128)} %get-tuple-element.155.dx_ref, ...), custom_call_target="tpu_custom_call" | custom-call | flops 3623878656 | bytes 15728640 | tf_op jit(solution)/shard_map/input_grad/pallas_call | solution.py:605
  263.9 2.8 collective-permute-done.17.d
  266.9 2.0 collective-permute-start.18
  268.9 5.9 %qkv_weight.1 = (bf16[8,64,768]{2,1,0:T(8,128)(2,1)}, bf16[8,64,768]{2,1,0:T(8,128)(2,1)}) custom-call(s32[10]{0:T(128)} %stack.45.tab, bf16[1024,768]{1,0:T(8,128)(2,1)} %get-tuple-element.118.x_ref.h_ref, bf16[3,1024,256]{2,1,0:T(8,128)(2,1)} %attend_back.3.da_ref.d_ref, f32[8,768]{1,0:T(8,128)} %get-tuple-element.166.din, ...), custom_call_target="tpu_custom_call" | custom-call | flops 1207959552 | bytes 3145728 | tf_op jit(solution)/shard_map/qkv_weight/pallas_call | solution.py:517
  274.8 2.3 collective-permute-done.18
  277.1 2.5 collective-permute-done.20
  279.6 1.1 copy-done.1
  280.8 1.5 collective-permute-start.21
  282.4 0.9 reshape.80
  283.3 6.7 %finish.2.refs_0_ = bf16[1024,768]{1,0:T(8,128)(2,1)} custom-call(bf16[1024,3072]{1,0:T(8,128)(2,1)} %get-tuple-element.176.act_ref, f32[1024,768]{1,0:T(8,128)} %get-tuple-element.129.refs_4_.x1_ref, bf16[16,432,768]{2,1,0:T(8,128)(2,1)} %bitcast.32, f32[1,7680]{1,0:T(1,128)} %get-tuple-element.109.biases.refs_9_.c2), custom_call_target="tpu_custom_call" | custom-call | flops 2415919104 | bytes 7864320 | tf_op jit(solution)/shard_map/finish/pallas_call | solution.py:326
  289.9 2.2 collective-permute-done.21.b
  292.2 0.7 collective-permute-start.22
  292.9 3.7 %collective-permute-start.23 = (bf16[64,768]{1,0:T(8,128)(2,1)S(1)}, bf16[64,768]{1,0:T(8,128)(2,1)S(1)}, u32[]{:S(2)}, u32[]{:S(2)}) collective-permute-start(bf16[64,768]{1,0:T(8,128)(2,1)S(1)} %get-tuple-element.187), channel_id=1, source_target_pairs={{0,16},{8,24},{16,0},{24,8},{1,17},{9,25},{17,1},{25,9},{2,18},{10... | collective-permute-start | bytes 294920 | tf_op jit(solution)/shard_map/ppermute | solution.py:762
  296.6 6.7 %finish.3 = bf16[1024,768]{1,0:T(8,128)(2,1)} custom-call(bf16[1024,3072]{1,0:T(8,128)(2,1)} %get-tuple-element.176.act_ref, f32[1024,768]{1,0:T(8,128)} %get-tuple-element.129.refs_4_.x1_ref, bf16[16,432,768]{2,1,0:T(8,128)(2,1)} %bitcast.33, f32[1,7680]{1,0:T(1,128)} %get-tuple-element.109.biases.refs_9_.c2, ...), custom_call_target="tpu_custom_call", output_to_operand_aliasing={{}: (4, {})} | custom-call | flops 2415919104 | bytes 7864320 | tf_op jit(solution)/shard_map/finish/pallas_call | solution.py:326
  303.3 2.8 collective-permute-done.23.c
  306.1 2.3 collective-permute-done.24.d
  308.4 0.9 collective-permute-start.25
  309.4 0.9 copy.18
  310.3 1.2 collective-permute-start.26
  311.5 2.6 collective-permute-done.25
  314.2 0.7 slice.125
  314.8 0.5 slice_bitcast_fusion
  315.3 1.9 collective-permute-done.26
  317.4 0.7 reshape.79
  318.1 0.8 reshape.78
  (94 shorter events, 2.5 us)
Async XLA Ops:
  7.2 4.4 %copy-start.12 = (bf16[480]{0:T(512)(128)(2,1)S(1)}, bf16[480]{0:T(512)(128)(2,1)}, u32[]{:S(2)}) copy-start(bf16[480]{0:T(512)(128)(2,1)} %param.15) | copy-start | bytes 2884
  7.2 4.4 %copy-start.13 = (bf16[96]{0:T(256)(128)(2,1)S(1)}, bf16[96]{0:T(256)(128)(2,1)}, u32[]{:S(2)}) copy-start(bf16[96]{0:T(256)(128)(2,1)} %param.14) | copy-start | bytes 580
  7.2 4.5 %copy-start.11 = (bf16[110592]{0:T(1024)(128)(2,1)S(1)}, bf16[110592]{0:T(1024)(128)(2,1)}, u32[]{:S(2)}) copy-start(bf16[110592]{0:T(1024)(128)(2,1)} %param.10) | copy-start | bytes 663556
  7.2 104.1 %all-gather.3.cloned.1.call-start = ((), (), s32[]{:S(2)}) async-start(), calls=%async_computation.4 | async-start | bytes 10948608 | tf_op jit(solution)/shard_map/all_gather | solution.py:854
  11.5 255.2 %reduce-scatter.3.cloned.1.call-start = ((), (), s32[]{:S(2)}) async-start(), calls=%async_computation.2 | async-start | bytes 5013504 | tf_op jit(solution)/shard_map/reduce_scatter | solution.py:877
  12.0 9.9 %collective-permute-start.2 = (bf16[64,768]{1,0:T(8,128)(2,1)S(1)}, bf16[64,768]{1,0:T(8,128)(2,1)S(1)}, u32[]{:S(2)}, u32[]{:S(2)}) collective-permute-start(bf16[64,768]{1,0:T(8,128)(2,1)S(1)} %fusion.1.refs_0_), channel_id=1, source_target_pairs={{0,24},{8,16},{16,8},{24,0},{1,25},{9,17},{17,9},{25,1},{2,26},{10... | collective-permute-start | bytes 294920 | tf_op jit(solution)/shard_map/ppermute | solution.py:762
  12.5 9.4 %collective-permute-start.1 = (bf16[64,768]{1,0:T(8,128)(2,1)S(1)}, bf16[64,768]{1,0:T(8,128)(2,1)S(1)}, u32[]{:S(2)}, u32[]{:S(2)}) collective-permute-start(bf16[64,768]{1,0:T(8,128)(2,1)S(1)} %fusion.1.refs_0_), channel_id=1, source_target_pairs={{0,16},{8,24},{16,0},{24,8},{1,17},{9,25},{17,1},{25,9},{2,18},{10... | collective-permute-start | bytes 294920 | tf_op jit(solution)/shard_map/ppermute | solution.py:762
  16.0 5.9 %collective-permute-start = (bf16[64,768]{1,0:T(8,128)(2,1)S(1)}, bf16[64,768]{1,0:T(8,128)(2,1)S(1)}, u32[]{:S(2)}, u32[]{:S(2)}) collective-permute-start(bf16[64,768]{1,0:T(8,128)(2,1)S(1)} %fusion.1.refs_0_), channel_id=1, source_target_pairs={{0,8},{8,0},{16,24},{24,16},{1,9},{9,1},{17,25},{25,17},{2,10},{10... | collective-permute-start | bytes 294920 | tf_op jit(solution)/shard_map/ppermute | solution.py:762
  21.9 17.4 %copy-start = (bf16[4,64,768]{2,1,0:T(8,128)(2,1)}, bf16[4,64,768]{2,1,0:T(8,128)(2,1)S(1)}, u32[]{:S(2)}) copy-start(bf16[4,64,768]{2,1,0:T(8,128)(2,1)S(1)} %stack.46.p0.a0) | copy-start | bytes 1179652
  21.9 1.8 collective-permute-start.4
  22.0 12.8 %collective-permute-start.3 = (bf16[4,64,768]{2,1,0:T(8,128)(2,1)S(1)}, bf16[4,64,768]{2,1,0:T(8,128)(2,1)S(1)}, u32[]{:S(2)}, u32[]{:S(2)}) collective-permute-start(bf16[4,64,768]{2,1,0:T(8,128)(2,1)S(1)} %stack.46.p0.a0), channel_id=1, source_target_pairs={{0,4},{4,0},{1,5},{5,1},{2,6},{6,2},{3,7},{7,3},{8,12},{12,8},{9,1... | collective-permute-start | bytes 1179656 | tf_op jit(solution)/shard_map/ppermute | solution.py:762
  23.7 15.6 %copy-start.6 = (bf16[4,64,768]{2,1,0:T(8,128)(2,1)}, bf16[4,64,768]{2,1,0:T(8,128)(2,1)S(1)}, u32[]{:S(2)}) copy-start(bf16[4,64,768]{2,1,0:T(8,128)(2,1)S(1)} %collective-permute-done.4.p2.a2) | copy-start | bytes 1179652
  34.8 4.5 %copy-start.7 = (bf16[4,64,768]{2,1,0:T(8,128)(2,1)}, bf16[4,64,768]{2,1,0:T(8,128)(2,1)S(1)}, u32[]{:S(2)}) copy-start(bf16[4,64,768]{2,1,0:T(8,128)(2,1)S(1)} %collective-permute-done.3.p1.a1) | copy-start | bytes 1179652
  34.8 4.5 %collective-permute-start.5 = (bf16[4,64,768]{2,1,0:T(8,128)(2,1)S(1)}, bf16[4,64,768]{2,1,0:T(8,128)(2,1)S(1)}, u32[]{:S(2)}, u32[]{:S(2)}) collective-permute-start(bf16[4,64,768]{2,1,0:T(8,128)(2,1)S(1)} %collective-permute-done.3.p1.a1), channel_id=1, source_target_pairs={{0,2},{2,0},{1,3},{3,1},{4,6},{6,4},{5,7},{7,5},{8,10},{10,8},{9,1... | collective-permute-start | bytes 1179656 | tf_op jit(solution)/shard_map/ppermute | solution.py:762
  34.8 17.7 %collective-permute-start.8 = (bf16[48,1536]{1,0:T(8,128)(2,1)S(1)}, bf16[48,1536]{1,0:T(8,128)(2,1)S(1)}, u32[]{:S(2)}, u32[]{:S(2)}) collective-permute-start(bf16[48,1536]{1,0:T(8,128)(2,1)S(1)} %pad_maximum_fusion.refs_0_), channel_id=1, source_target_pairs={{0,24},{8,16},{16,8},{24,0},{1,25},{9,17},{17,9},{25,1},{2,26},{10... | collective-permute-start | bytes 442376 | tf_op jit(solution)/shard_map/ppermute | solution.py:762
  35.4 24.1 %collective-permute-start.7 = (bf16[48,1536]{1,0:T(8,128)(2,1)S(1)}, bf16[48,1536]{1,0:T(8,128)(2,1)S(1)}, u32[]{:S(2)}, u32[]{:S(2)}) collective-permute-start(bf16[48,1536]{1,0:T(8,128)(2,1)S(1)} %pad_maximum_fusion.refs_0_), channel_id=1, source_target_pairs={{0,16},{8,24},{16,0},{24,8},{1,17},{9,25},{17,1},{25,9},{2,18},{10... | collective-permute-start | bytes 442376 | tf_op jit(solution)/shard_map/ppermute | solution.py:762
  38.7 20.8 %collective-permute-start.6 = (bf16[48,1536]{1,0:T(8,128)(2,1)S(1)}, bf16[48,1536]{1,0:T(8,128)(2,1)S(1)}, u32[]{:S(2)}, u32[]{:S(2)}) collective-permute-start(bf16[48,1536]{1,0:T(8,128)(2,1)S(1)} %pad_maximum_fusion.refs_0_), channel_id=1, source_target_pairs={{0,8},{8,0},{16,24},{24,16},{1,9},{9,1},{17,25},{25,17},{2,10},{10... | collective-permute-start | bytes 442376 | tf_op jit(solution)/shard_map/ppermute | solution.py:762
  39.4 0.7 copy-start.8
  59.6 12.8 %copy-start.2 = (bf16[4,48,1536]{2,1,0:T(8,128)(2,1)}, bf16[4,48,1536]{2,1,0:T(8,128)(2,1)S(1)}, u32[]{:S(2)}) copy-start(bf16[4,48,1536]{2,1,0:T(8,128)(2,1)S(1)} %stack.47.p0.b0) | copy-start | bytes 1769476
  59.6 12.8 %collective-permute-start.10 = (bf16[4,48,1536]{2,1,0:T(8,128)(2,1)S(1)}, bf16[4,48,1536]{2,1,0:T(8,128)(2,1)S(1)}, u32[]{:S(2)}, u32[]{:S(2)}) collective-permute-start(bf16[4,48,1536]{2,1,0:T(8,128)(2,1)S(1)} %stack.47.p0.b0), channel_id=1, source_target_pairs={{0,2},{2,0},{1,3},{3,1},{4,6},{6,4},{5,7},{7,5},{8,10},{10,8},{9,1... | collective-permute-start | bytes 1769480 | tf_op jit(solution)/shard_map/ppermute | solution.py:762
  59.7 18.9 %collective-permute-start.9 = (bf16[4,48,1536]{2,1,0:T(8,128)(2,1)S(1)}, bf16[4,48,1536]{2,1,0:T(8,128)(2,1)S(1)}, u32[]{:S(2)}, u32[]{:S(2)}) collective-permute-start(bf16[4,48,1536]{2,1,0:T(8,128)(2,1)S(1)} %stack.47.p0.b0), channel_id=1, source_target_pairs={{0,4},{4,0},{1,5},{5,1},{2,6},{6,2},{3,7},{7,3},{8,12},{12,8},{9,1... | collective-permute-start | bytes 1769480 | tf_op jit(solution)/shard_map/ppermute | solution.py:762
  72.4 8.1 %copy-start.14 = (bf16[4,48,1536]{2,1,0:T(8,128)(2,1)}, bf16[4,48,1536]{2,1,0:T(8,128)(2,1)S(1)}, u32[]{:S(2)}) copy-start(bf16[4,48,1536]{2,1,0:T(8,128)(2,1)S(1)} %collective-permute-done.10.p2.b2) | copy-start | bytes 1769476
  78.5 2.0 copy-start.15
  78.5 2.0 collective-permute-start.11
  80.5 0.9 copy-start.16
  153.5 154.8 %reduce-scatter.5.cloned.1.call-start = ((), (), s32[]{:S(2)}) async-start(), calls=%async_computation.3 | async-start | bytes 3760128 | tf_op jit(solution)/shard_map/reduce_scatter | solution.py:888
  169.6 10.6 %collective-permute-start.12 = (bf16[8,48,3072]{2,1,0:T(8,128)(2,1)}, bf16[8,48,3072]{2,1,0:T(8,128)(2,1)S(1)}, u32[]{:S(2)}, u32[]{:S(2)}) collective-permute-start(bf16[8,48,3072]{2,1,0:T(8,128)(2,1)} %get-tuple-element.131), channel_id=1, source_target_pairs={{0,2},{2,0},{1,3},{3,1},{4,6},{6,4},{5,7},{7,5},{8,10},{10,8},{9,1... | collective-permute-start | bytes 7077896 | tf_op jit(solution)/shard_map/ppermute | solution.py:762
  180.2 1.4 copy-start.4
  186.6 30.9 %collective-permute-start.13 = (bf16[8,48,1536]{2,1,0:T(8,128)(2,1)}, bf16[8,48,1536]{2,1,0:T(8,128)(2,1)S(1)}, u32[]{:S(2)}, u32[]{:S(2)}) collective-permute-start(bf16[8,48,1536]{2,1,0:T(8,128)(2,1)} %get-tuple-element.138), channel_id=1, source_target_pairs={{0,1},{1,0},{2,3},{3,2},{4,5},{5,4},{6,7},{7,6},{8,9},{9,8},{10,11... | collective-permute-start | bytes 3538952 | tf_op jit(solution)/shard_map/ppermute | solution.py:762
  217.5 7.6 %copy-start.5 = (bf16[8,48,1536]{2,1,0:T(8,128)(2,1)}, bf16[8,48,1536]{2,1,0:T(8,128)(2,1)S(1)}, u32[]{:S(2)}) copy-start(bf16[8,48,1536]{2,1,0:T(8,128)(2,1)S(1)} %collective-permute-done.13) | copy-start | bytes 3538948
  228.7 17.4 %collective-permute-start.14 = (bf16[4,48,1536]{2,1,0:T(8,128)(2,1)}, bf16[4,48,1536]{2,1,0:T(8,128)(2,1)S(1)}, u32[]{:S(2)}, u32[]{:S(2)}) collective-permute-start(bf16[4,48,1536]{2,1,0:T(8,128)(2,1)} %get-tuple-element.146), channel_id=1, source_target_pairs={{0,4},{4,0},{1,5},{5,1},{2,6},{6,2},{3,7},{7,3},{8,12},{12,8},{9,1... | collective-permute-start | bytes 1769480 | tf_op jit(solution)/shard_map/ppermute | solution.py:762
  229.6 16.5 %copy-start.3 = (bf16[4,48,1536]{2,1,0:T(8,128)(2,1)S(1)}, bf16[4,48,1536]{2,1,0:T(8,128)(2,1)}, u32[]{:S(2)}) copy-start(bf16[4,48,1536]{2,1,0:T(8,128)(2,1)} %get-tuple-element.140.a) | copy-start | bytes 1769476
  246.2 17.7 %collective-permute-start.15 = (bf16[48,1536]{1,0:T(8,128)(2,1)S(1)}, bf16[48,1536]{1,0:T(8,128)(2,1)S(1)}, u32[]{:S(2)}, u32[]{:S(2)}) collective-permute-start(bf16[48,1536]{1,0:T(8,128)(2,1)S(1)} %get-tuple-element.157), channel_id=1, source_target_pairs={{0,8},{8,0},{16,24},{24,16},{1,9},{9,1},{17,25},{25,17},{2,10},{10... | collective-permute-start | bytes 442376 | tf_op jit(solution)/shard_map/ppermute | solution.py:762
  250.5 13.3 %collective-permute-start.16 = (bf16[48,1536]{1,0:T(8,128)(2,1)S(1)}, bf16[48,1536]{1,0:T(8,128)(2,1)S(1)}, u32[]{:S(2)}, u32[]{:S(2)}) collective-permute-start(bf16[48,1536]{1,0:T(8,128)(2,1)S(1)} %get-tuple-element.158), channel_id=1, source_target_pairs={{0,16},{8,24},{16,0},{24,8},{1,17},{9,25},{17,1},{25,9},{2,18},{10... | collective-permute-start | bytes 442376 | tf_op jit(solution)/shard_map/ppermute | solution.py:762
  252.2 14.5 %collective-permute-start.17 = (bf16[48,1536]{1,0:T(8,128)(2,1)S(1)}, bf16[48,1536]{1,0:T(8,128)(2,1)S(1)}, u32[]{:S(2)}, u32[]{:S(2)}) collective-permute-start(bf16[48,1536]{1,0:T(8,128)(2,1)S(1)} %get-tuple-element.159), channel_id=1, source_target_pairs={{0,24},{8,16},{16,8},{24,0},{1,25},{9,17},{17,9},{25,1},{2,26},{10... | collective-permute-start | bytes 442376 | tf_op jit(solution)/shard_map/ppermute | solution.py:762
  266.8 10.3 %collective-permute-start.19 = (bf16[192,768]{1,0:T(8,128)(2,1)}, bf16[192,768]{1,0:T(8,128)(2,1)S(1)}, u32[]{:S(2)}, u32[]{:S(2)}) collective-permute-start(bf16[192,768]{1,0:T(8,128)(2,1)} %reduce-scatter.3.cloned.1.call-done), channel_id=1, source_target_pairs={{0,1},{1,0},{2,3},{3,2},{4,5},{5,4},{6,7},{7,6},{8,9},{9,8},{10,11... | collective-permute-start | bytes 884744 | tf_op jit(solution)/shard_map/ppermute | solution.py:762
  266.9 10.2 %collective-permute-start.18 = (bf16[48,1536]{1,0:T(8,128)(2,1)S(1)}, bf16[48,1536]{1,0:T(8,128)(2,1)S(1)}, u32[]{:S(2)}, u32[]{:S(2)}) collective-permute-start(bf16[48,1536]{1,0:T(8,128)(2,1)S(1)} %add_four.2), channel_id=1, source_target_pairs={{0,1},{1,0},{2,3},{3,2},{4,5},{5,4},{6,7},{7,6},{8,9},{9,8},{10,11... | collective-permute-start | bytes 442376 | tf_op jit(solution)/shard_map/ppermute | solution.py:762
  268.9 13.5 %copy-start.9 = (bf16[192,768]{1,0:T(8,128)(2,1)S(1)}, bf16[192,768]{1,0:T(8,128)(2,1)}, u32[]{:S(2)}) copy-start(bf16[192,768]{1,0:T(8,128)(2,1)} %reduce-scatter.3.cloned.1.call-done) | copy-start | bytes 884740
  277.1 2.5 collective-permute-start.20
  279.6 1.1 copy-start.1
  280.8 11.4 %collective-permute-start.21 = (bf16[4,64,768]{2,1,0:T(8,128)(2,1)S(1)}, bf16[4,64,768]{2,1,0:T(8,128)(2,1)S(1)}, u32[]{:S(2)}, u32[]{:S(2)}) collective-permute-start(bf16[4,64,768]{2,1,0:T(8,128)(2,1)S(1)} %get-tuple-element.178), channel_id=1, source_target_pairs={{0,4},{4,0},{1,5},{5,1},{2,6},{6,2},{3,7},{7,3},{8,12},{12,8},{9,1... | collective-permute-start | bytes 1179656 | tf_op jit(solution)/shard_map/ppermute | solution.py:762
  292.2 11.1 %collective-permute-start.22 = (bf16[64,768]{1,0:T(8,128)(2,1)S(1)}, bf16[64,768]{1,0:T(8,128)(2,1)S(1)}, u32[]{:S(2)}, u32[]{:S(2)}) collective-permute-start(bf16[64,768]{1,0:T(8,128)(2,1)S(1)} %get-tuple-element.186), channel_id=1, source_target_pairs={{0,8},{8,0},{16,24},{24,16},{1,9},{9,1},{17,25},{25,17},{2,10},{10... | collective-permute-start | bytes 294920 | tf_op jit(solution)/shard_map/ppermute | solution.py:762
  292.9 13.2 %collective-permute-start.23 = (bf16[64,768]{1,0:T(8,128)(2,1)S(1)}, bf16[64,768]{1,0:T(8,128)(2,1)S(1)}, u32[]{:S(2)}, u32[]{:S(2)}) collective-permute-start(bf16[64,768]{1,0:T(8,128)(2,1)S(1)} %get-tuple-element.187), channel_id=1, source_target_pairs={{0,16},{8,24},{16,0},{24,8},{1,17},{9,25},{17,1},{25,9},{2,18},{10... | collective-permute-start | bytes 294920 | tf_op jit(solution)/shard_map/ppermute | solution.py:762
  296.6 11.7 %collective-permute-start.24 = (bf16[64,768]{1,0:T(8,128)(2,1)S(1)}, bf16[64,768]{1,0:T(8,128)(2,1)S(1)}, u32[]{:S(2)}, u32[]{:S(2)}) collective-permute-start(bf16[64,768]{1,0:T(8,128)(2,1)S(1)} %get-tuple-element.188), channel_id=1, source_target_pairs={{0,24},{8,16},{16,8},{24,0},{1,25},{9,17},{17,9},{25,1},{2,26},{10... | collective-permute-start | bytes 294920 | tf_op jit(solution)/shard_map/ppermute | solution.py:762
  308.4 1.9 copy-start.10
  308.4 5.7 %collective-permute-start.25 = (bf16[64,768]{1,0:T(8,128)(2,1)S(1)}, bf16[64,768]{1,0:T(8,128)(2,1)S(1)}, u32[]{:S(2)}, u32[]{:S(2)}) collective-permute-start(bf16[64,768]{1,0:T(8,128)(2,1)S(1)} %add_four.3), channel_id=1, source_target_pairs={{0,1},{1,0},{2,3},{3,2},{4,5},{5,4},{6,7},{7,6},{8,9},{9,8},{10,11... | collective-permute-start | bytes 294920 | tf_op jit(solution)/shard_map/ppermute | solution.py:762
  310.3 7.0 %collective-permute-start.26 = (bf16[48,2304]{1,0:T(8,128)(2,1)S(1)}, bf16[48,2304]{1,0:T(8,128)(2,1)S(1)}, u32[]{:S(2)}, u32[]{:S(2)}) collective-permute-start(bf16[48,2304]{1,0:T(8,128)(2,1)S(1)} %copy-done.10), channel_id=1, source_target_pairs={{0,1},{1,0},{2,3},{3,2},{4,5},{5,4},{6,7},{7,6},{8,9},{9,8},{10,11... | collective-permute-start | bytes 663560 | tf_op jit(solution)/shard_map/ppermute | solution.py:762
Sparse Core Ops, SparseCore 0:
  11.6 99.5 all-gather.2
  153.6 78.4 reduce-scatter.2
  236.0 70.4 reduce-scatter.4
where the time goes:
time: 330 us; the launch traced here: 325 us
  Pallas kernels  212 us (64%)
  waiting for transfers between devices  55.9 us (17%)
  starting transfers between devices  29.3 us (9%)
  between operations  14.1 us (4%)
  local copies, waits for them, and re-layouts  13.8 us (4%)
    ppermute x27, waiting for transfers between devices, flip(): return lax.ppermute(value, axis, [(i, i ^ by) for i in range(size)])  54.8 us
    pallas_call x2, Pallas kernels, attend_back_call(): pl.pallas_call(functools.partial(attend_back_body, min(512, tokens)), gri...  45.9 us
    pallas_call x2, Pallas kernels, attend_call(): pl.pallas_call(functools.partial(attend_body, min(512, tokens)), grid=(pa...  34 us
    ppermute x27, starting transfers between devices, flip(): return lax.ppermute(value, axis, [(i, i ^ by) for i in range(size)])  29.2 us
    pallas_call x1, Pallas kernels, up_call(): pl.pallas_call(functools.partial(up_body, len(outs)), grid=(tokens // row...  25.4 us
    pallas_call x1, Pallas kernels, down_call(): pl.pallas_call(down_body, grid=(FF // D,), in_specs=[ff, ff, pl.BlockSpec...  16.8 us
    pallas_call x1, Pallas kernels, hidden_call(): pl.pallas_call(hidden_body, grid_spec=pltpu.PrefetchScalarGridSpec(num_sc...  16.1 us
    pallas_call x2, Pallas kernels, qkv_call(): pl.pallas_call(functools.partial(qkv_body, first, at), grid_spec=pltpu.Pr...  14.1 us
  transfers between devices with their start and end apart: 30, of which 16 were waited for; matrix products, arithmetic and copies ran while one was open for 1% of the time, Pallas kernels for 52%

commit v1 on v0

--- a/solution.py
+++ b/solution.py
@@ -112,7 +112,7 @@
             def block(r):
                 h_ref[r, :] = layer_norm(x_ref[r, :].astype(F32), gain[...], biases[:, :D]).astype(B16)
 
-            each_block(x_ref.shape[0], 256, block)
+            each_block(x_ref.shape[0], 32, block)
 
         h = h_ref
     else:
@@ -150,8 +150,12 @@
     )(tab, x, *parts, gains, biases)
 
 
-def each_block(count, rows, run):
+def each_block(count, rows, run, unroll=False):
     rows = min(rows, count)
+    if unroll:
+        for b in range(count // rows):
+            run(slice(b * rows, (b + 1) * rows))
+        return
 
     def step(b, carry):
         run(pl.ds(pl.multiple_of(b * rows, rows), rows))
@@ -171,7 +175,7 @@
         each_block(seg_ref.shape[1], 128, block)
 
 
-def attend_body(rows, q_ref, k_ref, v_ref, seg_ref, o_ref, lse_ref, mask):
+def attend_body(rows, unroll, q_ref, k_ref, v_ref, seg_ref, o_ref, lse_ref, mask):
     make_mask(seg_ref, mask)
 
     def block(r):
@@ -185,16 +189,16 @@
             o_ref[r, cols] = (mm(p.astype(B16), v_ref[0, :, cols], 1, 0) * (1.0 / total)).astype(B16)
             lse_ref[0, h : h + 1, r] = (top + jnp.log(total)).T
 
-    each_block(q_ref.shape[1], rows, block)
-
-
-def attend_call(qkv, seg, start=0, pairs=None):
+    each_block(q_ref.shape[1], rows, block, unroll)
+
+
+def attend_call(qkv, seg, rows, unroll=False, start=0, pairs=None):
     _, tokens, width = qkv.shape
     pairs = pairs or width // 128
     width = pairs * 128
     head = lambda j: pl.BlockSpec((1, tokens, 128), lambda i: (j, 0, i + start))
     return pl.pallas_call(
-        functools.partial(attend_body, min(512, tokens)),
+        functools.partial(attend_body, min(rows, tokens), unroll),
         grid=(pairs,),
         in_specs=[head(0), head(1), head(2), pl.BlockSpec((1, tokens), lambda i: (0, 0))],
         out_specs=[
@@ -282,7 +286,7 @@
         du_ref[r, :] = du
         dc1[...] += jnp.sum(du.astype(F32), axis=0, keepdims=True)
 
-    each_block(dy_ref.shape[0], 512, block)
+    each_block(dy_ref.shape[0], 512, block, True)
     dw_ref[...] = mm(act_ref[...], dy_ref[...], 0, 0).astype(B16)
 
 
@@ -865,11 +869,11 @@
     qkv0, z1 = tie(qkv0, z1)
     a1 = stack([s1, *z1])
     x1, c1 = along_x(a1), across(a1)
-    o0, lse0 = attend_call(qkv0, seg)
+    o0, lse0 = attend_call(qkv0, seg, 128)
     o0, x1, c1, h1 = tie(o0, x1, c1, h1)
     w1 = (a1, x1, c1, across(x1))
     (qkv1,) = qkv_call(False, starts[1], tab, h1, w1, gain_all, bias_all)
-    o1, lse1 = attend_call(qkv1, seg)
+    o1, lse1 = attend_call(qkv1, seg, 512, True)
     outs = [o0, o1]
     x1, h2, act, slope = up_call(outs, tokens, bulk, gain_all, bias_all)
 
@@ -959,8 +963,8 @@
     starts = [a for a, _ in bounds_of()]
     qkv0, h1 = qkv_call(True, starts[0], tab, tokens, w0, gain_all, bias_all)
     (qkv1,) = qkv_call(False, starts[1], tab, h1, w1, gain_all, bias_all)
-    o0, lse0 = attend_call(qkv0, seg)
-    o1, lse1 = attend_call(qkv1, seg)
+    o0, lse0 = attend_call(qkv0, seg, 128)
+    o1, lse1 = attend_call(qkv1, seg, 512, True)
     outs = [o0, o1]
     x1, h2, act, slope = up_call(outs, tokens, bulk, gain_all, bias_all)
     output = finish_call(act, x1, bulk, bias_all, 0, 4)

time: 330 us -> 326 us (0.988)
  waiting for transfers between devices: 55.9 us -> 47.6 us
  Pallas kernels: 212 us -> 220 us
  starting transfers between devices: 29.3 us -> 25.9 us
    ppermute x27, waiting for transfers between devices: 54.8 us -> 45.4 us  [flip(): return lax.ppermute(value, axis, [(i, i ^ by) for i in range(size)])]
    pallas_call x2, Pallas kernels: 34 us -> 38.8 us  [attend_call(): pl.pallas_call(functools.partial(attend_body, min(rows, tokens), unroll),...]
    pallas_call x2, Pallas kernels: 14.1 us -> 18.8 us  [qkv_call(): pl.pallas_call(functools.partial(qkv_body, first, at), grid_spec=pltpu.Pr...]
    ppermute x27, starting transfers between devices: 29.2 us -> 25.8 us  [flip(): return lax.ppermute(value, axis, [(i, i ^ by) for i in range(size)])]
  transfers between devices with their start and end apart: 30 -> 30, of which waited for: 16 -> 14; matrix products, arithmetic and copies ran while one was open for 1% -> 1% of each run, Pallas kernels for 52% -> 56%
where the time goes in v1:
time: 326 us; the launch traced here: 322 us
  Pallas kernels  220 us (67%)
  waiting for transfers between devices  47.6 us (15%)
  starting transfers between devices  25.9 us (8%)
  between operations  14.2 us (4%)
  local copies, waits for them, and re-layouts  13.8 us (4%)
    pallas_call x2, Pallas kernels, attend_back_call(): pl.pallas_call(functools.partial(attend_back_body, min(512, tokens)), gri...  45.9 us
    ppermute x27, waiting for transfers between devices, flip(): return lax.ppermute(value, axis, [(i, i ^ by) for i in range(size)])  45.4 us
    pallas_call x2, Pallas kernels, attend_call(): pl.pallas_call(functools.partial(attend_body, min(rows, tokens), unroll),...  38.8 us
    ppermute x27, starting transfers between devices, flip(): return lax.ppermute(value, axis, [(i, i ^ by) for i in range(size)])  25.8 us
    pallas_call x1, Pallas kernels, up_call(): pl.pallas_call(functools.partial(up_body, len(outs)), grid=(tokens // row...  25.4 us
    pallas_call x2, Pallas kernels, qkv_call(): pl.pallas_call(functools.partial(qkv_body, first, at), grid_spec=pltpu.Pr...  18.8 us
    pallas_call x1, Pallas kernels, hidden_call(): pl.pallas_call(hidden_body, grid_spec=pltpu.PrefetchScalarGridSpec(num_sc...  16.1 us
    pallas_call x1, Pallas kernels, down_call(): pl.pallas_call(down_body, grid=(FF // D,), in_specs=[ff, ff, pl.BlockSpec...  15.4 us
  transfers between devices with their start and end apart: 30, of which 14 were waited for; matrix products, arithmetic and copies ran while one was open for 1% of the time, Pallas kernels for 56%

profile of v1, /device:TPU:16, one launch (start us, length us, event | category | flops | bytes accessed | tf_op | source)
XLA Modules:
  0.0 322.2 jit_solution(14806873084006135177)
XLA Ops:
  7.2 1.0 reshape.72
  8.3 1.1 reshape.71
  9.4 1.2 reshape.70
  10.7 0.8 constant_dynamic-slice_fusion
  11.7 0.3 reshape.67
  12.0 0.5 collective-permute-start.2
  12.5 3.5 %collective-permute-start.1 = (bf16[64,768]{1,0:T(8,128)(2,1)S(1)}, bf16[64,768]{1,0:T(8,128)(2,1)S(1)}, u32[]{:S(2)}, u32[]{:S(2)}) collective-permute-start(bf16[64,768]{1,0:T(8,128)(2,1)S(1)} %fusion.1.refs_0_), channel_id=1, source_target_pairs={{0,16},{8,24},{16,0},{24,8},{1,17},{9,25},{17,1},{25,9},{2,18},{10... | collective-permute-start | bytes 294920 | tf_op jit(solution)/shard_map/ppermute | solution.py:766
  16.0 5.9 %collective-permute-done.2.refs_3_ = bf16[64,768]{1,0:T(8,128)(2,1)S(1)} collective-permute-done((bf16[64,768]{1,0:T(8,128)(2,1)S(1)}, bf16[64,768]{1,0:T(8,128)(2,1)S(1)}, u32[]{:S(2)}, u32[]{:S(2)}) %collective-permute-start.2) | collective-permute-done | bytes 98336 | tf_op jit(solution)/shard_map/ppermute | solution.py:766
  22.0 1.6 collective-permute-start.3
  23.7 11.1 %collective-permute-done.3.p1.a1 = bf16[4,64,768]{2,1,0:T(8,128)(2,1)S(1)} collective-permute-done((bf16[4,64,768]{2,1,0:T(8,128)(2,1)S(1)}, bf16[4,64,768]{2,1,0:T(8,128)(2,1)S(1)}, u32[]{:S(2)}, u32[]{:S(2)}) %collective-permute-start.3) | collective-permute-done | bytes 393248 | tf_op jit(solution)/shard_map/ppermute | solution.py:766
  34.8 0.6 collective-permute-start.8
  35.4 3.3 %collective-permute-start.7 = (bf16[48,1536]{1,0:T(8,128)(2,1)S(1)}, bf16[48,1536]{1,0:T(8,128)(2,1)S(1)}, u32[]{:S(2)}, u32[]{:S(2)}) collective-permute-start(bf16[48,1536]{1,0:T(8,128)(2,1)S(1)} %pad_maximum_fusion.refs_0_), channel_id=1, source_target_pairs={{0,16},{8,24},{16,0},{24,8},{1,17},{9,25},{17,1},{25,9},{2,18},{10... | collective-permute-start | bytes 442376 | tf_op jit(solution)/shard_map/ppermute | solution.py:766
  38.7 0.7 stack.45.tab
  39.4 0.7 copy-done.8
  40.1 2.5 vectors.1
  42.6 11.6 %qkv_first.1 = (bf16[3,1024,256]{2,1,0:T(8,128)(2,1)}, bf16[1024,768]{1,0:T(8,128)(2,1)}) custom-call(s32[10]{0:T(128)} %stack.45.tab, bf16[1024,768]{1,0:T(8,128)(2,1)} %x_ref.3, bf16[4,64,768]{2,1,0:T(8,128)(2,1)} %copy-done, bf16[4,64,768]{2,1,0:T(8,128)(2,1)} %copy-done.7, bf16[4,64,768]{2,1,0:T(8,128)(2,1)} %copy-done.6, bf16[4,64,768]{2,1,0:T(8,128)(2,1)} %copy-done.8, ...), custom_call_target="tpu_custom_call" | custom-call | flops 1207959552 | bytes 6291456 | tf_op jit(solution)/shard_map/qkv_first/pallas_call | solution.py:137
  54.2 5.3 %collective-permute-done.7.refs_2_ = bf16[48,1536]{1,0:T(8,128)(2,1)S(1)} collective-permute-done((bf16[48,1536]{1,0:T(8,128)(2,1)S(1)}, bf16[48,1536]{1,0:T(8,128)(2,1)S(1)}, u32[]{:S(2)}, u32[]{:S(2)}) %collective-permute-start.7) | collective-permute-done | bytes 147488 | tf_op jit(solution)/shard_map/ppermute | solution.py:766
  59.7 0.4 collective-permute-start.9
  60.0 20.1 %attend.2 = (bf16[1024,256]{1,0:T(8,128)(2,1)}, f32[2,2,1024]{2,1,0:T(2,128)}) custom-call(bf16[3,1024,256]{2,1,0:T(8,128)(2,1)} %get-tuple-element.112.q_ref.k_ref.v_ref, bf16[3,1024,256]{2,1,0:T(8,128)(2,1)} %get-tuple-element.112.q_ref.k_ref.v_ref, bf16[3,1024,256]{2,1,0:T(8,128)(2,1)} %get-tuple-element.112.q_ref.k_ref.v_ref, s32[1,1024]{1,0:T(1,128)} %bitcast.38), custom_call_target="tpu_custom_call" | custom-call | flops 4294967296 | bytes 2097152 | tf_op jit(solution)/shard_map/attend/pallas_call | solution.py:200
  80.2 0.2 collective-permute-start.11
  80.4 1.9 collective-permute-done.11.p3.b3
  82.3 0.9 copy-done.16
  83.2 7.2 %qkv_next.1.q_ref.k_ref.v_ref = bf16[3,1024,512]{2,1,0:T(8,128)(2,1)} custom-call(s32[10]{0:T(128)} %stack.45.tab, bf16[1024,768]{1,0:T(8,128)(2,1)} %get-tuple-element.118.x_ref.h_ref, bf16[4,48,1536]{2,1,0:T(8,128)(2,1)} %copy-done.2, bf16[4,48,1536]{2,1,0:T(8,128)(2,1)} %copy-done.15, bf16[4,48,1536]{2,1,0:T(8,128)(2,1)} %copy-done.14, ...), custom_call_target="tpu_custom_call" | custom-call | flops 2415919104 | bytes 6291456 | tf_op jit(solution)/shard_map/qkv_next/pallas_call | solution.py:137
  90.4 18.8 %attend.3 = (bf16[1024,512]{1,0:T(8,128)(2,1)}, f32[4,2,1024]{2,1,0:T(2,128)}) custom-call(bf16[3,1024,512]{2,1,0:T(8,128)(2,1)} %qkv_next.1.q_ref.k_ref.v_ref, bf16[3,1024,512]{2,1,0:T(8,128)(2,1)} %qkv_next.1.q_ref.k_ref.v_ref, bf16[3,1024,512]{2,1,0:T(8,128)(2,1)} %qkv_next.1.q_ref.k_ref.v_ref, s32[1,1024]{1,0:T(1,128)} %bitcast.39), custom_call_target="tpu_custom_call" | custom-call | flops 8589934592 | bytes 4194304 | tf_op jit(solution)/shard_map/attend/pallas_call | solution.py:200
  109.1 2.1 all-gather.3.cloned.1.call-done
  111.3 25.4 %up.1 = (f32[1024,768]{1,0:T(8,128)}, bf16[1024,768]{1,0:T(8,128)(2,1)}, bf16[1024,3072]{1,0:T(8,128)(2,1)}, bf16[1024,3072]{1,0:T(8,128)(2,1)}) custom-call(bf16[1024,256]{1,0:T(8,128)(2,1)} %get-tuple-element.119.refs_0_.o_ref, bf16[1024,512]{1,0:T(8,128)(2,1)} %get-tuple-element.122.refs_1_.o_ref, bf16[1024,768]{1,0:T(8,128)(2,1)} %x_ref.3, ...), custom_call_target="tpu_custom_call" | custom-call | flops 6039797760 | bytes 23592960 | tf_op jit(solution)/shard_map/up/pallas_call | solution.py:261
  136.7 15.4 %down.1 = (bf16[1024,3072]{1,0:T(8,128)(2,1)}, bf16[3072,768]{1,0:T(8,128)(2,1)}, f32[1,3072]{1,0:T(1,128)}, f32[1,768]{1,0:T(1,128)}) custom-call(bf16[1024,3072]{1,0:T(8,128)(2,1)} %get-tuple-element.176.act_ref, bf16[1024,3072]{1,0:T(8,128)(2,1)} %get-tuple-element.125.slope_ref, bf16[1024,768]{1,0:T(8,128)(2,1)} %refs_3_.1, bf16[16,432,768]{2,1,0:T(8,128)(2,1)} %bitcast.29), custom_call_target="tpu_custom_call" | custom-call | flops 9663676416 | bytes 23592960 | tf_op jit(solution)/shard_map/down/pallas_call | solution.py:296
  152.2 16.1 %hidden.1 = (f32[1024,768]{1,0:T(8,128)}, bf16[8,48,3072]{2,1,0:T(8,128)(2,1)}, bf16[8,48,3072]{2,1,0:T(8,128)(2,1)}) custom-call(s32[10]{0:T(128)} %stack.45.tab, bf16[1024,768]{1,0:T(8,128)(2,1)} %get-tuple-element.123.h2_ref, bf16[1024,3072]{1,0:T(8,128)(2,1)} %get-tuple-element.126.du_ref, bf16[16,432,768]{2,1,0:T(8,128)(2,1)} %bitcast.30), custom_call_target="tpu_custom_call" | custom-call | flops 9663676416 | bytes 15728640 | tf_op jit(solution)/shard_map/hidden/pallas_call | solution.py:365
  168.3 0.3 collective-permute-start.12
  168.6 10.2 %middle.1 = (f32[1024,768]{1,0:T(8,128)}, bf16[1024,768]{1,0:T(8,128)(2,1)}, bf16[768,768]{1,0:T(8,128)(2,1)}, f32[8,768]{1,0:T(8,128)}) custom-call(bf16[1024,256]{1,0:T(8,128)(2,1)} %get-tuple-element.119.refs_0_.o_ref, bf16[1024,512]{1,0:T(8,128)(2,1)} %get-tuple-element.122.refs_1_.o_ref, f32[1024,768]{1,0:T(8,128)} %get-tuple-element.128.refs_2_, ...), custom_call_target="tpu_custom_call" | custom-call | flops 2415919104 | bytes 15728640 | tf_op jit(solution)/shard_map/middle/pallas_call | solution.py:417
  178.8 1.4 copy-done.4
  180.2 5.4 %add_halves.1 = (bf16[8,48,1536]{2,1,0:T(8,128)(2,1)}, bf16[8,48,1536]{2,1,0:T(8,128)(2,1)}) custom-call(s32[10]{0:T(128)} %stack.45.tab, bf16[8,48,3072]{2,1,0:T(8,128)(2,1)} %get-tuple-element.127.a0.a1, bf16[8,48,3072]{2,1,0:T(8,128)(2,1)} %copy-done.4, bf16[8,48,3072]{2,1,0:T(8,128)(2,1)} %get-tuple-element.127.a0.a1, bf16[8,48,3072]{2,1,0:T(8,128)(2,1)} %copy-done.4), custom_call_target="tpu_custom_call" | custom-call | flops 1179648 | bytes 7077888 | tf_op jit(solution)/shard_map/add_halves/pallas_call | solution.py:684
  185.6 1.5 collective-permute-start.13
  187.0 29.4 %attend_back.2.d_ref.db_ref = bf16[3,1024,512]{2,1,0:T(8,128)(2,1)} custom-call(bf16[3,1024,512]{2,1,0:T(8,128)(2,1)} %qkv_next.1.q_ref.k_ref.v_ref, bf16[3,1024,512]{2,1,0:T(8,128)(2,1)} %qkv_next.1.q_ref.k_ref.v_ref, bf16[3,1024,512]{2,1,0:T(8,128)(2,1)} %qkv_next.1.q_ref.k_ref.v_ref, bf16[1024,768]{1,0:T(8,128)(2,1)} %get-tuple-element.144.do_ref, ...), custom_call_target="tpu_custom_call" | custom-call | flops 21474836480 | bytes 8388608 | tf_op jit(solution)/shard_map/attend_back/pallas_call | solution.py:465
  216.5 7.5 %joint_weight.1 = bf16[768,2304]{1,0:T(8,128)(2,1)} custom-call(bf16[1024,768]{1,0:T(8,128)(2,1)} %get-tuple-element.118.x_ref.h_ref, bf16[3,1024,512]{2,1,0:T(8,128)(2,1)} %attend_back.2.d_ref.db_ref, bf16[768,768]{1,0:T(8,128)(2,1)} %get-tuple-element.142.o_ref), custom_call_target="tpu_custom_call" | custom-call | flops 2415919104 | bytes 6291456 | tf_op jit(solution)/shard_map/joint_weight/pallas_call | solution.py:554
  224.0 3.7 %add_split.2 = (bf16[4,48,1536]{2,1,0:T(8,128)(2,1)}, bf16[4,48,1536]{2,1,0:T(8,128)(2,1)}) custom-call(bf16[2,4,48,1536]{3,2,1,0:T(8,128)(2,1)} %bitcast.34, bf16[2,4,48,1536]{3,2,1,0:T(8,128)(2,1)} %bitcast.35), custom_call_target="tpu_custom_call" | custom-call | flops 589824 | bytes 3538944 | tf_op jit(solution)/shard_map/add_split/pallas_call | solution.py:665
  227.7 16.5 %attend_back.3.da_ref.d_ref = bf16[3,1024,256]{2,1,0:T(8,128)(2,1)} custom-call(bf16[3,1024,256]{2,1,0:T(8,128)(2,1)} %get-tuple-element.112.q_ref.k_ref.v_ref, bf16[3,1024,256]{2,1,0:T(8,128)(2,1)} %get-tuple-element.112.q_ref.k_ref.v_ref, bf16[3,1024,256]{2,1,0:T(8,128)(2,1)} %get-tuple-element.112.q_ref.k_ref.v_ref, ...), custom_call_target="tpu_custom_call" | custom-call | flops 10737418240 | bytes 4194304 | tf_op jit(solution)/shard_map/attend_back/pallas_call | solution.py:465
  244.3 3.4 %collective-permute-start.15 = (bf16[48,1536]{1,0:T(8,128)(2,1)S(1)}, bf16[48,1536]{1,0:T(8,128)(2,1)S(1)}, u32[]{:S(2)}, u32[]{:S(2)}) collective-permute-start(bf16[48,1536]{1,0:T(8,128)(2,1)S(1)} %get-tuple-element.157), channel_id=1, source_target_pairs={{0,8},{8,0},{16,24},{24,16},{1,9},{9,1},{17,25},{25,17},{2,10},{10... | collective-permute-start | bytes 442376 | tf_op jit(solution)/shard_map/ppermute | solution.py:766
  247.8 1.5 collective-permute-start.17
  249.2 11.1 %input_grad.1 = (f32[1024,768]{1,0:T(8,128)}, f32[8,768]{1,0:T(8,128)}) custom-call(s32[10]{0:T(128)} %stack.45.tab, bf16[3,1024,256]{2,1,0:T(8,128)(2,1)} %attend_back.3.da_ref.d_ref, bf16[3,1024,512]{2,1,0:T(8,128)(2,1)} %attend_back.2.d_ref.db_ref, bf16[1024,768]{1,0:T(8,128)(2,1)} %x_ref.3, f32[1024,768]{1,0:T(8,128)} %get-tuple-element.155.dx_ref, ...), custom_call_target="tpu_custom_call" | custom-call | flops 3623878656 | bytes 15728640 | tf_op jit(solution)/shard_map/input_grad/pallas_call | solution.py:609
  260.4 3.6 %collective-permute-done.17.d = bf16[48,1536]{1,0:T(8,128)(2,1)S(1)} collective-permute-done((bf16[48,1536]{1,0:T(8,128)(2,1)S(1)}, bf16[48,1536]{1,0:T(8,128)(2,1)S(1)}, u32[]{:S(2)}, u32[]{:S(2)}) %collective-permute-start.17) | collective-permute-done | bytes 147488 | tf_op jit(solution)/shard_map/ppermute | solution.py:766
  264.2 2.0 collective-permute-start.18
  266.2 5.9 %qkv_weight.1 = (bf16[8,64,768]{2,1,0:T(8,128)(2,1)}, bf16[8,64,768]{2,1,0:T(8,128)(2,1)}) custom-call(s32[10]{0:T(128)} %stack.45.tab, bf16[1024,768]{1,0:T(8,128)(2,1)} %get-tuple-element.118.x_ref.h_ref, bf16[3,1024,256]{2,1,0:T(8,128)(2,1)} %attend_back.3.da_ref.d_ref, f32[8,768]{1,0:T(8,128)} %get-tuple-element.166.din, ...), custom_call_target="tpu_custom_call" | custom-call | flops 1207959552 | bytes 3145728 | tf_op jit(solution)/shard_map/qkv_weight/pallas_call | solution.py:521
  272.1 1.4 collective-permute-done.18
  273.5 2.5 collective-permute-done.20
  276.0 1.1 copy-done.1
  277.2 0.9 collective-permute-start.21
  278.2 0.9 reshape.80
  279.0 6.7 %finish.2.refs_0_ = bf16[1024,768]{1,0:T(8,128)(2,1)} custom-call(bf16[1024,3072]{1,0:T(8,128)(2,1)} %get-tuple-element.176.act_ref, f32[1024,768]{1,0:T(8,128)} %get-tuple-element.129.refs_4_.x1_ref, bf16[16,432,768]{2,1,0:T(8,128)(2,1)} %bitcast.32, f32[1,7680]{1,0:T(1,128)} %get-tuple-element.109.biases.refs_9_.c2), custom_call_target="tpu_custom_call" | custom-call | flops 2415919104 | bytes 7864320 | tf_op jit(solution)/shard_map/finish/pallas_call | solution.py:330
  285.7 2.7 collective-permute-done.21.b
  288.5 1.1 collective-permute-start.22
  289.6 2.7 collective-permute-start.23
  292.3 6.6 %finish.3 = bf16[1024,768]{1,0:T(8,128)(2,1)} custom-call(bf16[1024,3072]{1,0:T(8,128)(2,1)} %get-tuple-element.176.act_ref, f32[1024,768]{1,0:T(8,128)} %get-tuple-element.129.refs_4_.x1_ref, bf16[16,432,768]{2,1,0:T(8,128)(2,1)} %bitcast.33, f32[1,7680]{1,0:T(1,128)} %get-tuple-element.109.biases.refs_9_.c2, ...), custom_call_target="tpu_custom_call", output_to_operand_aliasing={{}: (4, {})} | custom-call | flops 2415919104 | bytes 7864320 | tf_op jit(solution)/shard_map/finish/pallas_call | solution.py:330
  299.0 3.3 %collective-permute-done.23.c = bf16[64,768]{1,0:T(8,128)(2,1)S(1)} collective-permute-done((bf16[64,768]{1,0:T(8,128)(2,1)S(1)}, bf16[64,768]{1,0:T(8,128)(2,1)S(1)}, u32[]{:S(2)}, u32[]{:S(2)}) %collective-permute-start.23) | collective-permute-done | bytes 98336 | tf_op jit(solution)/shard_map/ppermute | solution.py:766
  302.2 2.6 collective-permute-done.24.d
  304.8 0.8 collective-permute-start.25
  305.8 0.9 copy.18
  306.7 1.2 collective-permute-start.26
  307.9 2.6 collective-permute-done.25
  310.6 0.7 slice.125
  311.3 0.5 slice_bitcast_fusion
  311.8 2.3 collective-permute-done.26
  314.1 0.7 reshape.79
  314.9 0.8 reshape.78
  (94 shorter events, 1.6 us)
Async XLA Ops:
  7.2 4.4 %copy-start.12 = (bf16[480]{0:T(512)(128)(2,1)S(1)}, bf16[480]{0:T(512)(128)(2,1)}, u32[]{:S(2)}) copy-start(bf16[480]{0:T(512)(128)(2,1)} %param.15) | copy-start | bytes 2884
  7.2 4.4 %copy-start.13 = (bf16[96]{0:T(256)(128)(2,1)S(1)}, bf16[96]{0:T(256)(128)(2,1)}, u32[]{:S(2)}) copy-start(bf16[96]{0:T(256)(128)(2,1)} %param.14) | copy-start | bytes 580
  7.2 4.5 %copy-start.11 = (bf16[110592]{0:T(1024)(128)(2,1)S(1)}, bf16[110592]{0:T(1024)(128)(2,1)}, u32[]{:S(2)}) copy-start(bf16[110592]{0:T(1024)(128)(2,1)} %param.10) | copy-start | bytes 663556
  7.2 104.1 %all-gather.3.cloned.1.call-start = ((), (), s32[]{:S(2)}) async-start(), calls=%async_computation.4 | async-start | bytes 10948608 | tf_op jit(solution)/shard_map/all_gather | solution.py:858
  11.5 252.5 %reduce-scatter.3.cloned.1.call-start = ((), (), s32[]{:S(2)}) async-start(), calls=%async_computation.2 | async-start | bytes 5013504 | tf_op jit(solution)/shard_map/reduce_scatter | solution.py:881
  12.0 9.9 %collective-permute-start.2 = (bf16[64,768]{1,0:T(8,128)(2,1)S(1)}, bf16[64,768]{1,0:T(8,128)(2,1)S(1)}, u32[]{:S(2)}, u32[]{:S(2)}) collective-permute-start(bf16[64,768]{1,0:T(8,128)(2,1)S(1)} %fusion.1.refs_0_), channel_id=1, source_target_pairs={{0,24},{8,16},{16,8},{24,0},{1,25},{9,17},{17,9},{25,1},{2,26},{10... | collective-permute-start | bytes 294920 | tf_op jit(solution)/shard_map/ppermute | solution.py:766
  12.5 9.4 %collective-permute-start.1 = (bf16[64,768]{1,0:T(8,128)(2,1)S(1)}, bf16[64,768]{1,0:T(8,128)(2,1)S(1)}, u32[]{:S(2)}, u32[]{:S(2)}) collective-permute-start(bf16[64,768]{1,0:T(8,128)(2,1)S(1)} %fusion.1.refs_0_), channel_id=1, source_target_pairs={{0,16},{8,24},{16,0},{24,8},{1,17},{9,25},{17,1},{25,9},{2,18},{10... | collective-permute-start | bytes 294920 | tf_op jit(solution)/shard_map/ppermute | solution.py:766
  16.0 5.9 %collective-permute-start = (bf16[64,768]{1,0:T(8,128)(2,1)S(1)}, bf16[64,768]{1,0:T(8,128)(2,1)S(1)}, u32[]{:S(2)}, u32[]{:S(2)}) collective-permute-start(bf16[64,768]{1,0:T(8,128)(2,1)S(1)} %fusion.1.refs_0_), channel_id=1, source_target_pairs={{0,8},{8,0},{16,24},{24,16},{1,9},{9,1},{17,25},{25,17},{2,10},{10... | collective-permute-start | bytes 294920 | tf_op jit(solution)/shard_map/ppermute | solution.py:766
  21.9 17.4 %copy-start = (bf16[4,64,768]{2,1,0:T(8,128)(2,1)}, bf16[4,64,768]{2,1,0:T(8,128)(2,1)S(1)}, u32[]{:S(2)}) copy-start(bf16[4,64,768]{2,1,0:T(8,128)(2,1)S(1)} %stack.46.p0.a0) | copy-start | bytes 1179652
  21.9 1.8 collective-permute-start.4
  22.0 12.8 %collective-permute-start.3 = (bf16[4,64,768]{2,1,0:T(8,128)(2,1)S(1)}, bf16[4,64,768]{2,1,0:T(8,128)(2,1)S(1)}, u32[]{:S(2)}, u32[]{:S(2)}) collective-permute-start(bf16[4,64,768]{2,1,0:T(8,128)(2,1)S(1)} %stack.46.p0.a0), channel_id=1, source_target_pairs={{0,4},{4,0},{1,5},{5,1},{2,6},{6,2},{3,7},{7,3},{8,12},{12,8},{9,1... | collective-permute-start | bytes 1179656 | tf_op jit(solution)/shard_map/ppermute | solution.py:766
  23.7 15.6 %copy-start.6 = (bf16[4,64,768]{2,1,0:T(8,128)(2,1)}, bf16[4,64,768]{2,1,0:T(8,128)(2,1)S(1)}, u32[]{:S(2)}) copy-start(bf16[4,64,768]{2,1,0:T(8,128)(2,1)S(1)} %collective-permute-done.4.p2.a2) | copy-start | bytes 1179652
  34.8 4.5 %copy-start.7 = (bf16[4,64,768]{2,1,0:T(8,128)(2,1)}, bf16[4,64,768]{2,1,0:T(8,128)(2,1)S(1)}, u32[]{:S(2)}) copy-start(bf16[4,64,768]{2,1,0:T(8,128)(2,1)S(1)} %collective-permute-done.3.p1.a1) | copy-start | bytes 1179652
  34.8 4.5 %collective-permute-start.5 = (bf16[4,64,768]{2,1,0:T(8,128)(2,1)S(1)}, bf16[4,64,768]{2,1,0:T(8,128)(2,1)S(1)}, u32[]{:S(2)}, u32[]{:S(2)}) collective-permute-start(bf16[4,64,768]{2,1,0:T(8,128)(2,1)S(1)} %collective-permute-done.3.p1.a1), channel_id=1, source_target_pairs={{0,2},{2,0},{1,3},{3,1},{4,6},{6,4},{5,7},{7,5},{8,10},{10,8},{9,1... | collective-permute-start | bytes 1179656 | tf_op jit(solution)/shard_map/ppermute | solution.py:766
  34.8 19.4 %collective-permute-start.8 = (bf16[48,1536]{1,0:T(8,128)(2,1)S(1)}, bf16[48,1536]{1,0:T(8,128)(2,1)S(1)}, u32[]{:S(2)}, u32[]{:S(2)}) collective-permute-start(bf16[48,1536]{1,0:T(8,128)(2,1)S(1)} %pad_maximum_fusion.refs_0_), channel_id=1, source_target_pairs={{0,24},{8,16},{16,8},{24,0},{1,25},{9,17},{17,9},{25,1},{2,26},{10... | collective-permute-start | bytes 442376 | tf_op jit(solution)/shard_map/ppermute | solution.py:766
  35.4 24.1 %collective-permute-start.7 = (bf16[48,1536]{1,0:T(8,128)(2,1)S(1)}, bf16[48,1536]{1,0:T(8,128)(2,1)S(1)}, u32[]{:S(2)}, u32[]{:S(2)}) collective-permute-start(bf16[48,1536]{1,0:T(8,128)(2,1)S(1)} %pad_maximum_fusion.refs_0_), channel_id=1, source_target_pairs={{0,16},{8,24},{16,0},{24,8},{1,17},{9,25},{17,1},{25,9},{2,18},{10... | collective-permute-start | bytes 442376 | tf_op jit(solution)/shard_map/ppermute | solution.py:766
  38.7 20.8 %collective-permute-start.6 = (bf16[48,1536]{1,0:T(8,128)(2,1)S(1)}, bf16[48,1536]{1,0:T(8,128)(2,1)S(1)}, u32[]{:S(2)}, u32[]{:S(2)}) collective-permute-start(bf16[48,1536]{1,0:T(8,128)(2,1)S(1)} %pad_maximum_fusion.refs_0_), channel_id=1, source_target_pairs={{0,8},{8,0},{16,24},{24,16},{1,9},{9,1},{17,25},{25,17},{2,10},{10... | collective-permute-start | bytes 442376 | tf_op jit(solution)/shard_map/ppermute | solution.py:766
  39.4 0.7 copy-start.8
  59.6 20.6 %copy-start.2 = (bf16[4,48,1536]{2,1,0:T(8,128)(2,1)}, bf16[4,48,1536]{2,1,0:T(8,128)(2,1)S(1)}, u32[]{:S(2)}) copy-start(bf16[4,48,1536]{2,1,0:T(8,128)(2,1)S(1)} %stack.47.p0.b0) | copy-start | bytes 1769476
  59.6 20.5 %collective-permute-start.10 = (bf16[4,48,1536]{2,1,0:T(8,128)(2,1)S(1)}, bf16[4,48,1536]{2,1,0:T(8,128)(2,1)S(1)}, u32[]{:S(2)}, u32[]{:S(2)}) collective-permute-start(bf16[4,48,1536]{2,1,0:T(8,128)(2,1)S(1)} %stack.47.p0.b0), channel_id=1, source_target_pairs={{0,2},{2,0},{1,3},{3,1},{4,6},{6,4},{5,7},{7,5},{8,10},{10,8},{9,1... | collective-permute-start | bytes 1769480 | tf_op jit(solution)/shard_map/ppermute | solution.py:766
  59.7 20.5 %collective-permute-start.9 = (bf16[4,48,1536]{2,1,0:T(8,128)(2,1)S(1)}, bf16[4,48,1536]{2,1,0:T(8,128)(2,1)S(1)}, u32[]{:S(2)}, u32[]{:S(2)}) collective-permute-start(bf16[4,48,1536]{2,1,0:T(8,128)(2,1)S(1)} %stack.47.p0.b0), channel_id=1, source_target_pairs={{0,4},{4,0},{1,5},{5,1},{2,6},{6,2},{3,7},{7,3},{8,12},{12,8},{9,1... | collective-permute-start | bytes 1769480 | tf_op jit(solution)/shard_map/ppermute | solution.py:766
  80.1 2.1 copy-start.14
  80.1 2.1 copy-start.15
  80.2 2.1 collective-permute-start.11
  82.3 0.9 copy-start.16
  152.2 152.6 %reduce-scatter.5.cloned.1.call-start = ((), (), s32[]{:S(2)}) async-start(), calls=%async_computation.3 | async-start | bytes 3760128 | tf_op jit(solution)/shard_map/reduce_scatter | solution.py:892
  168.3 10.5 %collective-permute-start.12 = (bf16[8,48,3072]{2,1,0:T(8,128)(2,1)}, bf16[8,48,3072]{2,1,0:T(8,128)(2,1)S(1)}, u32[]{:S(2)}, u32[]{:S(2)}) collective-permute-start(bf16[8,48,3072]{2,1,0:T(8,128)(2,1)} %get-tuple-element.131), channel_id=1, source_target_pairs={{0,2},{2,0},{1,3},{3,1},{4,6},{6,4},{5,7},{7,5},{8,10},{10,8},{9,1... | collective-permute-start | bytes 7077896 | tf_op jit(solution)/shard_map/ppermute | solution.py:766
  178.8 1.4 copy-start.4
  185.6 30.9 %collective-permute-start.13 = (bf16[8,48,1536]{2,1,0:T(8,128)(2,1)}, bf16[8,48,1536]{2,1,0:T(8,128)(2,1)S(1)}, u32[]{:S(2)}, u32[]{:S(2)}) collective-permute-start(bf16[8,48,1536]{2,1,0:T(8,128)(2,1)} %get-tuple-element.138), channel_id=1, source_target_pairs={{0,1},{1,0},{2,3},{3,2},{4,5},{5,4},{6,7},{7,6},{8,9},{9,8},{10,11... | collective-permute-start | bytes 3538952 | tf_op jit(solution)/shard_map/ppermute | solution.py:766
  216.4 7.5 %copy-start.5 = (bf16[8,48,1536]{2,1,0:T(8,128)(2,1)}, bf16[8,48,1536]{2,1,0:T(8,128)(2,1)S(1)}, u32[]{:S(2)}) copy-start(bf16[8,48,1536]{2,1,0:T(8,128)(2,1)S(1)} %collective-permute-done.13) | copy-start | bytes 3538948
  227.7 16.5 %collective-permute-start.14 = (bf16[4,48,1536]{2,1,0:T(8,128)(2,1)}, bf16[4,48,1536]{2,1,0:T(8,128)(2,1)S(1)}, u32[]{:S(2)}, u32[]{:S(2)}) collective-permute-start(bf16[4,48,1536]{2,1,0:T(8,128)(2,1)} %get-tuple-element.146), channel_id=1, source_target_pairs={{0,4},{4,0},{1,5},{5,1},{2,6},{6,2},{3,7},{7,3},{8,12},{12,8},{9,1... | collective-permute-start | bytes 1769480 | tf_op jit(solution)/shard_map/ppermute | solution.py:766
  227.7 16.5 %copy-start.3 = (bf16[4,48,1536]{2,1,0:T(8,128)(2,1)S(1)}, bf16[4,48,1536]{2,1,0:T(8,128)(2,1)}, u32[]{:S(2)}) copy-start(bf16[4,48,1536]{2,1,0:T(8,128)(2,1)} %get-tuple-element.140.a) | copy-start | bytes 1769476
  244.3 16.1 %collective-permute-start.15 = (bf16[48,1536]{1,0:T(8,128)(2,1)S(1)}, bf16[48,1536]{1,0:T(8,128)(2,1)S(1)}, u32[]{:S(2)}, u32[]{:S(2)}) collective-permute-start(bf16[48,1536]{1,0:T(8,128)(2,1)S(1)} %get-tuple-element.157), channel_id=1, source_target_pairs={{0,8},{8,0},{16,24},{24,16},{1,9},{9,1},{17,25},{25,17},{2,10},{10... | collective-permute-start | bytes 442376 | tf_op jit(solution)/shard_map/ppermute | solution.py:766
  247.7 12.7 %collective-permute-start.16 = (bf16[48,1536]{1,0:T(8,128)(2,1)S(1)}, bf16[48,1536]{1,0:T(8,128)(2,1)S(1)}, u32[]{:S(2)}, u32[]{:S(2)}) collective-permute-start(bf16[48,1536]{1,0:T(8,128)(2,1)S(1)} %get-tuple-element.158), channel_id=1, source_target_pairs={{0,16},{8,24},{16,0},{24,8},{1,17},{9,25},{17,1},{25,9},{2,18},{10... | collective-permute-start | bytes 442376 | tf_op jit(solution)/shard_map/ppermute | solution.py:766
  247.8 16.2 %collective-permute-start.17 = (bf16[48,1536]{1,0:T(8,128)(2,1)S(1)}, bf16[48,1536]{1,0:T(8,128)(2,1)S(1)}, u32[]{:S(2)}, u32[]{:S(2)}) collective-permute-start(bf16[48,1536]{1,0:T(8,128)(2,1)S(1)} %get-tuple-element.159), channel_id=1, source_target_pairs={{0,24},{8,16},{16,8},{24,0},{1,25},{9,17},{17,9},{25,1},{2,26},{10... | collective-permute-start | bytes 442376 | tf_op jit(solution)/shard_map/ppermute | solution.py:766
  264.1 9.4 %collective-permute-start.19 = (bf16[192,768]{1,0:T(8,128)(2,1)}, bf16[192,768]{1,0:T(8,128)(2,1)S(1)}, u32[]{:S(2)}, u32[]{:S(2)}) collective-permute-start(bf16[192,768]{1,0:T(8,128)(2,1)} %reduce-scatter.3.cloned.1.call-done), channel_id=1, source_target_pairs={{0,1},{1,0},{2,3},{3,2},{4,5},{5,4},{6,7},{7,6},{8,9},{9,8},{10,11... | collective-permute-start | bytes 884744 | tf_op jit(solution)/shard_map/ppermute | solution.py:766
  264.2 9.3 %collective-permute-start.18 = (bf16[48,1536]{1,0:T(8,128)(2,1)S(1)}, bf16[48,1536]{1,0:T(8,128)(2,1)S(1)}, u32[]{:S(2)}, u32[]{:S(2)}) collective-permute-start(bf16[48,1536]{1,0:T(8,128)(2,1)S(1)} %add_four.2), channel_id=1, source_target_pairs={{0,1},{1,0},{2,3},{3,2},{4,5},{5,4},{6,7},{7,6},{8,9},{9,8},{10,11... | collective-permute-start | bytes 442376 | tf_op jit(solution)/shard_map/ppermute | solution.py:766
  266.2 11.9 %copy-start.9 = (bf16[192,768]{1,0:T(8,128)(2,1)S(1)}, bf16[192,768]{1,0:T(8,128)(2,1)}, u32[]{:S(2)}) copy-start(bf16[192,768]{1,0:T(8,128)(2,1)} %reduce-scatter.3.cloned.1.call-done) | copy-start | bytes 884740
  273.5 2.5 collective-permute-start.20
  276.0 1.1 copy-start.1
  277.2 11.2 %collective-permute-start.21 = (bf16[4,64,768]{2,1,0:T(8,128)(2,1)S(1)}, bf16[4,64,768]{2,1,0:T(8,128)(2,1)S(1)}, u32[]{:S(2)}, u32[]{:S(2)}) collective-permute-start(bf16[4,64,768]{2,1,0:T(8,128)(2,1)S(1)} %get-tuple-element.178), channel_id=1, source_target_pairs={{0,4},{4,0},{1,5},{5,1},{2,6},{6,2},{3,7},{7,3},{8,12},{12,8},{9,1... | collective-permute-start | bytes 1179656 | tf_op jit(solution)/shard_map/ppermute | solution.py:766
  288.5 10.5 %collective-permute-start.22 = (bf16[64,768]{1,0:T(8,128)(2,1)S(1)}, bf16[64,768]{1,0:T(8,128)(2,1)S(1)}, u32[]{:S(2)}, u32[]{:S(2)}) collective-permute-start(bf16[64,768]{1,0:T(8,128)(2,1)S(1)} %get-tuple-element.186), channel_id=1, source_target_pairs={{0,8},{8,0},{16,24},{24,16},{1,9},{9,1},{17,25},{25,17},{2,10},{10... | collective-permute-start | bytes 294920 | tf_op jit(solution)/shard_map/ppermute | solution.py:766
  289.6 12.6 %collective-permute-start.23 = (bf16[64,768]{1,0:T(8,128)(2,1)S(1)}, bf16[64,768]{1,0:T(8,128)(2,1)S(1)}, u32[]{:S(2)}, u32[]{:S(2)}) collective-permute-start(bf16[64,768]{1,0:T(8,128)(2,1)S(1)} %get-tuple-element.187), channel_id=1, source_target_pairs={{0,16},{8,24},{16,0},{24,8},{1,17},{9,25},{17,1},{25,9},{2,18},{10... | collective-permute-start | bytes 294920 | tf_op jit(solution)/shard_map/ppermute | solution.py:766
  292.3 12.5 %collective-permute-start.24 = (bf16[64,768]{1,0:T(8,128)(2,1)S(1)}, bf16[64,768]{1,0:T(8,128)(2,1)S(1)}, u32[]{:S(2)}, u32[]{:S(2)}) collective-permute-start(bf16[64,768]{1,0:T(8,128)(2,1)S(1)} %get-tuple-element.188), channel_id=1, source_target_pairs={{0,24},{8,16},{16,8},{24,0},{1,25},{9,17},{17,9},{25,1},{2,26},{10... | collective-permute-start | bytes 294920 | tf_op jit(solution)/shard_map/ppermute | solution.py:766
  304.8 1.9 copy-start.10
  304.8 5.7 %collective-permute-start.25 = (bf16[64,768]{1,0:T(8,128)(2,1)S(1)}, bf16[64,768]{1,0:T(8,128)(2,1)S(1)}, u32[]{:S(2)}, u32[]{:S(2)}) collective-permute-start(bf16[64,768]{1,0:T(8,128)(2,1)S(1)} %add_four.3), channel_id=1, source_target_pairs={{0,1},{1,0},{2,3},{3,2},{4,5},{5,4},{6,7},{7,6},{8,9},{9,8},{10,11... | collective-permute-start | bytes 294920 | tf_op jit(solution)/shard_map/ppermute | solution.py:766
  306.7 7.3 %collective-permute-start.26 = (bf16[48,2304]{1,0:T(8,128)(2,1)S(1)}, bf16[48,2304]{1,0:T(8,128)(2,1)S(1)}, u32[]{:S(2)}, u32[]{:S(2)}) collective-permute-start(bf16[48,2304]{1,0:T(8,128)(2,1)S(1)} %copy-done.10), channel_id=1, source_target_pairs={{0,1},{1,0},{2,3},{3,2},{4,5},{5,4},{6,7},{7,6},{8,9},{9,8},{10,11... | collective-permute-start | bytes 663560 | tf_op jit(solution)/shard_map/ppermute | solution.py:766
Sparse Core Ops, SparseCore 0:
  11.6 99.5 all-gather.2
  152.3 76.1 reduce-scatter.2
  232.3 70.4 reduce-scatter.4
